TPU v7x, 32 devices: a whole 2x2x4 slice. The times are simulated.
32 devices in a mesh: stem: 8 (over y, x, core), grp: 4 (over z).
Axes of the slice: x: 2, y: 2, z: 4, core: 2. Of those that a mesh axis runs over, the one named last changes fastest.
Arguments:
- stem_tensor: float32 [32, 512, 512], P(None, 'stem', 'grp'), may hold values from -6 to 6
- left_factors: float32 [2, 16, 16, 256], P(None, 'grp'), may hold values from -0.375 to 0.375
- right_factors: float32 [2, 256, 1024], replicated, may hold values from -0.1875 to 0.1875
- index_labels: int32 [2, 9], replicated, may hold values from 0 to 8, each once within a row
Outputs:
- contracted: float32 [32, 512, 512], P(('stem', 'grp'))
Inputs may be any that keep to these rules, and one draw needn't show every extreme that they name: `index_labels`: each row is a permutation of 0 to 8.
All inputs are finite; a program needn't handle non-finite values.
Results may differ from a plain program's by a relative error of at most 0.000098.
Values sent between devices are 32-bit elements; how exact they have to be, the bound alone decides.
No kernel may reach another device: no remote copies, remote signals or barrier semaphores. Data moves between devices by JAX's collectives and lax.ppermute only.
A program may use at most 64 MiB of HBM per device.

v0:
```python
import jax
import jax.numpy as jnp
from jax import lax
from jax.sharding import PartitionSpec as P

LOW = 32


def assemble(left, right):
    upper = left.shape[1]
    table = right.reshape(right.shape[0], LOW, LOW)
    product = jnp.einsum("abk,kcd->acbd", left, table, precision=lax.Precision.HIGHEST)
    return product.reshape(left.shape[0] * LOW, upper * LOW)


def relabel(branch, bit_order):
    row_ids = jnp.arange(branch.shape[0], dtype=jnp.int32)
    source_rows = jnp.zeros_like(row_ids)
    for bit_number in range(bit_order.shape[0]):
        picked = jnp.bitwise_and(jnp.right_shift(row_ids, bit_number), 1)
        source_rows = source_rows + jnp.left_shift(picked, bit_order[bit_number])
    return jnp.take(branch, source_rows, axis=0)


def contract_last(tensor, branch):
    dims = tensor.shape
    flat = jnp.dot(tensor.reshape(-1, dims[-1]), branch, precision=lax.Precision.HIGHEST)
    return flat.reshape(dims[:-1] + (branch.shape[1],))


def on_device(stem_tensor, left_factors, right_factors, index_labels):
    whole_left = lax.all_gather(left_factors, "grp", axis=1, tiled=True)
    branches = jnp.stack(
        [assemble(whole_left[branch_id], right_factors[branch_id]) for branch_id in range(2)]
    )
    branch_one = relabel(branches[0], index_labels[0])
    branch_two = relabel(branches[1], index_labels[1])
    stem_count = lax.axis_size("stem")
    open_rows, outer_local, inner_local = stem_tensor.shape
    shaped = stem_tensor.reshape(stem_count, open_rows // stem_count, outer_local, inner_local)
    regrouped = lax.all_to_all(shaped, "grp", split_axis=1, concat_axis=3, tiled=True)
    halfway = contract_last(regrouped, branch_one)
    gathered_modes = lax.all_to_all(halfway, "stem", split_axis=0, concat_axis=2, tiled=True)
    slab = gathered_modes[0]
    return lax.dot_general(
        slab, branch_two, (((1,), (0,)), ((), ())), precision=lax.Precision.HIGHEST
    )


def solution(mesh):
    placed = (P(None, "stem", "grp"), P(None, "grp", None, None), P(), P())
    return jax.shard_map(
        on_device,
        mesh=mesh,
        in_specs=placed,
        out_specs=P(("stem", "grp"), None, None),
        check_vma=False,
    )
```

profile of v0, /device:TPU:0, one launch (start us, length us, event | category | flops | bytes accessed | tf_op | source)
XLA Modules:
  0.0 91.7 jit_solution(12908365413325150748)
XLA Ops:
  0.0 2.3 %copy.20 = f32[8,4,64,128]{3,2,0,1:T(8,128)} copy(f32[8,4,64,128]{3,2,1,0:T(8,128)} %bitcast.70) | data formatting | bytes 2097152 | tf_op jit(solution)/shard_map/reshape | solution.py:40
  2.3 0.0 copy-start.2
  2.3 6.5 %all-to-all-start = ((f32[8,4,64,128]{3,2,0,1:T(8,128)}), f32[8,4,64,128]{3,2,0,1:T(8,128)S(1)}, u32[]{:S(2)}, u32[]{:S(2)}) async-start(f32[8,4,64,128]{3,2,0,1:T(8,128)} %copy.20), calls=%async_computation | async-start | bytes 2097152 | tf_op jit(solution)/shard_map/all_to_all | solution.py:41
  8.8 2.7 %fusion.11 = (f32[1,256,1024]{2,1,0:T(8,128)}, f32[1,256,1024]{2,1,0:T(8,128)S(1)}) fusion(f32[2,256,1024]{2,1,0:T(8,128)} %param.8), kind=kLoop, calls=%fused_computation.33 | loop fusion | bytes 4194304 | tf_op jit(solution)/shard_map/slice | solution.py:34
  11.5 0.3 copy.18
  11.8 0.0 copy-done.2
  11.8 33.1 %all_gather.3 = f32[2,16,16,256]{3,2,1,0:T(8,128)S(1)} all-gather(f32[2,4,16,256]{3,2,1,0:T(8,128)S(1)} %copy-done.2), channel_id=1, replica_groups=mesh['stem'=8,'grp'=4] {'grp'}, dimensions={1}, use_global_device_ids=true | all-gather | bytes 655360 | tf_op jit(solution)/shard_map/all_gather | solution.py:32
  44.9 0.0 copy-start.1
  44.9 0.8 copy-done.1
  45.7 3.4 %convolution_bitcast_fusion.1 = f32[16,32,16,32]{3,2,0,1:T(8,128)S(1)} fusion(f32[256,32,32,1]{0,2,3,1:T(8,128)S(1)} %bitcast.68, f32[2,16,16,256]{3,2,1,0:T(8,128)S(1)} %all_gather.3), kind=kOutput, calls=%fused_computation.3 | convolution fusion | flops 805306368 | bytes 2359296 | tf_op jit(solution)/shard_map/abk,kcd->acbd/dot_general | solution.py:12
  49.2 2.4 %copy.19 = f32[16,32,16,32]{3,2,1,0:T(8,128)} copy(f32[16,32,16,32]{3,2,0,1:T(8,128)S(1)} %convolution_bitcast_fusion.1) | data formatting | bytes 2097152 | tf_op jit(solution)/shard_map/abk,kcd->acbd/transpose | solution.py:12
  51.6 0.0 copy-start.3
  51.6 3.6 %squeeze_stack_reshape.6 = f32[512,512]{1,0:T(8,128)S(1)} reshape(f32[16,32,16,32]{3,2,1,0:T(8,128)} %copy.19) | data formatting | bytes 2097152 | tf_op jit(solution)/shard_map/squeeze;stack;reshape | solution.py:36
  55.1 0.0 copy-done.3
  55.2 0.7 fusion.12
  55.9 5.6 %compare_and_fusion.1 = (pred[512]{0:T(512)(128)(4,1)S(1)}, s32[512]{0:T(512)S(1)}) fusion(s32[]{:T(128)} %bitcast.8, s32[]{:T(128)} %bitcast.7, s32[]{:T(128)} %bitcast.6, s32[]{:T(128)} %bitcast.5, s32[]{:T(128)} %bitcast.4, s32[]{:T(128)} %bitcast.3, s32[]{:T(128)} %bitcast.2, s32[]{:T(128)} %bitcast.1, s32[]{:T(128)} %bitcast), kind=kLoop, calls=%fused_computation.30 | loop fusion | flops 20992 | bytes 2596 | tf_op jit(solution)/shard_map/jit(_take)/and | solution.py:22
  61.5 1.6 %gather_fusion = f32[512,512]{1,0:T(8,128)S(1)} fusion(f32[512,512]{1,0:T(8,128)S(1)} %squeeze_stack_reshape.6, s32[1024]{0:T(1024)S(1)} %pad_clamp_fusion.1), kind=kCustom, calls=%fused_computation.clone | custom fusion | bytes 2099200 | tf_op jit(solution)/shard_map/jit(_take)/gather | solution.py:22
  63.2 0.0 copy-start
  63.2 0.0 all-to-all-done
  63.2 0.7 copy.21
  63.9 3.0 %fusion = f32[512,512]{0,1:T(8,128)} fusion(f32[64,8,4,128]{3,2,1,0:T(4,128)S(1)} %bitcast.67, f32[512,512]{1,0:T(8,128)S(1)} %gather_fusion, pred[512]{0:T(512)(128)(4,1)S(1)} %get-tuple-element.8), kind=kOutput, calls=%fused_computation.5 | convolution fusion | flops 1610874880 | bytes 3146240 | tf_op jit(solution)/shard_map/dot_general | solution.py:27
  66.9 3.7 %all-to-all-start.1 = ((f32[8,1,64,512]{3,2,1,0:T(8,128)}), f32[8,1,64,512]{3,2,1,0:T(8,128)S(1)}, u32[]{:S(2)}, u32[]{:S(2)}) async-start(f32[8,1,64,512]{3,2,1,0:T(8,128)} %bitcast.20), calls=%async_computation.1 | async-start | bytes 2097152 | tf_op jit(solution)/shard_map/all_to_all | solution.py:43
  70.6 0.0 copy-done
  70.6 0.3 copy.23
  71.0 4.4 %convolution_bitcast_fusion = f32[16,32,16,32]{3,2,0,1:T(8,128)S(1)} fusion(f32[256,32,32,1]{0,2,3,1:T(8,128)S(1)} %bitcast.69, f32[2,16,16,256]{3,2,1,0:T(8,128)} %copy-done.1), kind=kOutput, calls=%fused_computation.2 | convolution fusion | flops 805306368 | bytes 2359296 | tf_op jit(solution)/shard_map/abk,kcd->acbd/dot_general | solution.py:12
  75.4 2.4 %copy.24 = f32[16,32,16,32]{3,2,1,0:T(8,128)} copy(f32[16,32,16,32]{3,2,0,1:T(8,128)S(1)} %convolution_bitcast_fusion) | data formatting | bytes 2097152 | tf_op jit(solution)/shard_map/abk,kcd->acbd/transpose | solution.py:12
  77.8 3.5 %squeeze_stack_reshape.7 = f32[512,512]{1,0:T(8,128)S(1)} reshape(f32[16,32,16,32]{3,2,1,0:T(8,128)} %copy.24) | data formatting | bytes 2097152 | tf_op jit(solution)/shard_map/squeeze;stack;reshape | solution.py:37
  81.3 5.6 %compare_and_fusion = (pred[512]{0:T(512)(128)(4,1)S(1)}, s32[512]{0:T(512)S(1)}) fusion(s32[]{:T(128)} %bitcast.30, s32[]{:T(128)} %bitcast.29, s32[]{:T(128)} %bitcast.28, s32[]{:T(128)} %bitcast.27, s32[]{:T(128)} %bitcast.26, s32[]{:T(128)} %bitcast.25, s32[]{:T(128)} %bitcast.24, s32[]{:T(128)} %bitcast.23, s32[]{:T(128)} %bitcast.22), kind=kLoop, calls=%fused_computation.29 | loop fusion | flops 20992 | bytes 2596 | tf_op jit(solution)/shard_map/jit(_take)/and | solution.py:22
  87.0 1.6 %gather_fusion.1 = f32[512,512]{1,0:T(8,128)S(1)} fusion(f32[512,512]{1,0:T(8,128)S(1)} %squeeze_stack_reshape.7, s32[1024]{0:T(1024)S(1)} %pad_clamp_fusion), kind=kCustom, calls=%fused_computation.1.clone | custom fusion | bytes 2099200 | tf_op jit(solution)/shard_map/jit(_take)/gather | solution.py:22
  88.6 0.0 all-to-all-done.1
  88.6 3.1 %convolution_bitcast_fusion.2 = f32[1,512,512]{2,1,0:T(8,128)} fusion(f32[512,512]{1,0:T(8,128)S(1)} %bitcast.66, f32[512,512]{1,0:T(8,128)S(1)} %gather_fusion.1, pred[512]{0:T(512)(128)(4,1)S(1)} %get-tuple-element.6), kind=kOutput, calls=%fused_computation.4 | convolution fusion | flops 1610874880 | bytes 3146240 | tf_op jit(solution)/shard_map/dot_general | solution.py:45
  (2 shorter events, 0.0 us)
Async XLA Ops:
  2.3 9.5 %copy-start.2 = (f32[2,4,16,256]{3,2,1,0:T(8,128)S(1)}, f32[2,4,16,256]{3,2,1,0:T(8,128)}, u32[]{:S(2)}) copy-start(f32[2,4,16,256]{3,2,1,0:T(8,128)} %param.7) | copy-start | bytes 393220
  2.3 60.9 %all-to-all-start = ((f32[8,4,64,128]{3,2,0,1:T(8,128)}), f32[8,4,64,128]{3,2,0,1:T(8,128)S(1)}, u32[]{:S(2)}, u32[]{:S(2)}) async-start(f32[8,4,64,128]{3,2,0,1:T(8,128)} %copy.20), calls=%async_computation | async-start | bytes 2097152 | tf_op jit(solution)/shard_map/all_to_all | solution.py:41
  44.9 0.8 copy-start.1
  51.6 3.6 %copy-start.3 = (s32[2,9]{1,0:T(2,128)S(1)}, s32[2,9]{1,0:T(2,128)}, u32[]{:S(2)}) copy-start(s32[2,9]{1,0:T(2,128)} %param.9) | copy-start | bytes 220
  63.2 7.5 %copy-start = (f32[1,256,1024]{2,1,0:T(8,128)S(1)}, f32[1,256,1024]{2,1,0:T(8,128)}, u32[]{:S(2)}) copy-start(f32[1,256,1024]{2,1,0:T(8,128)} %get-tuple-element.10) | copy-start | bytes 3145732
  66.9 21.7 %all-to-all-start.1 = ((f32[8,1,64,512]{3,2,1,0:T(8,128)}), f32[8,1,64,512]{3,2,1,0:T(8,128)S(1)}, u32[]{:S(2)}, u32[]{:S(2)}) async-start(f32[8,1,64,512]{3,2,1,0:T(8,128)} %bitcast.20), calls=%async_computation.1 | async-start | bytes 2097152 | tf_op jit(solution)/shard_map/all_to_all | solution.py:43
where the time goes:
time: 92.3 us; the launch traced here: 91.7 us
  blocking collectives  33.1 us (36%)
  local copies, waits for them, and re-layouts  23.1 us (25%)
  matrix products  13.9 us (15%)
  other arithmetic  11.3 us (12%)
  starting transfers between devices  10.2 us (11%)
    all_gather x1, blocking collectives, on_device(): whole_left = lax.all_gather(left_factors, 'grp', axis=1, tiled=True)  33.1 us
    and x2, other arithmetic, relabel(): return jnp.take(branch, source_rows, axis=0)  11.3 us
    dot_general x2, matrix products, assemble(): jnp.einsum('abk,kcd->acbd', left, table, precision=lax.Precision.HIGHEST)  7.84 us
    all_to_all x1, starting transfers between devices, on_device(): lax.all_to_all(shaped, 'grp', split_axis=1, concat_axis=3, tiled=True)  6.48 us
    transpose x2, local copies, waits for them, and re-layouts, assemble(): jnp.einsum('abk,kcd->acbd', left, table, precision=lax.Precision.HIGHEST)  4.82 us
    all_to_all x1, starting transfers between devices, on_device(): lax.all_to_all(halfway, 'stem', split_axis=0, concat_axis=2, tiled=True)  3.74 us
    another operation x1, local copies, waits for them, and re-layouts, on_device(): branch_one = relabel(branches[0], index_labels[0])  3.56 us
    another operation x1, local copies, waits for them, and re-layouts, on_device(): branch_two = relabel(branches[1], index_labels[1])  3.54 us
  transfers between devices with their start and end apart: 2, of which 0 were waited for; matrix products, arithmetic and copies ran while one was open for 42% of the time, Pallas kernels for 0%

commit v1 on v0

v1 whole, which is shorter than its diff:
```python
import functools
import jax
import jax.numpy as jnp
from jax import lax
from jax.experimental import pallas as pl
from jax.experimental.pallas import tpu as pltpu
from jax.sharding import PartitionSpec as P


LOW = 32
LANES = 128


def split(x):
    high = x.astype(jnp.bfloat16)
    low = (x - high.astype(jnp.float32)).astype(jnp.bfloat16)
    return high, low


def dot3(a, b, dims):
    (a_high, a_low), (b_high, b_low) = a, b

    def one(x, y):
        return lax.dot_general(x, y, (dims, ((), ())), preferred_element_type=jnp.float32)

    return one(a_high, b_high) + (one(a_high, b_low) + one(a_low, b_high))


def branch_kernel(stems, grps, place, labels, pieces, right, *refs):
    outs, (ordered, product, wide) = refs[:-3], refs[-3:]
    branches, u_part, p_part, _ = pieces.shape[2:]
    upper_u, upper_p = stems * u_part, grps * p_part
    rows = upper_p * LOW
    cols = upper_u * LOW
    per_lane = LANES // LOW
    lane_group = lax.broadcasted_iota(jnp.int32, (upper_p, LANES), 1) // LOW
    row_id = lax.broadcasted_iota(jnp.int32, (rows, 1), 0)
    col_id = lax.broadcasted_iota(jnp.int32, (rows, rows), 1)
    for b in range(branches):
        for s in range(stems):
            for g in range(grps):
                block = pieces[place[0] ^ s, place[1] ^ g, b]
                for u in range(u_part):
                    ordered[pl.ds((s * u_part + u) * upper_p + g * p_part, p_part), :] = block[u]
        product[...] = dot3(split(ordered[...]), split(right[b]), ((1,), (0,)))
        for c in range(LOW * LOW // LANES):
            for a in range(cols // LANES):
                tiles = [
                    product[pl.ds((a * per_lane + k) * upper_p, upper_p), pl.ds(c * LANES, LANES)]
                    for k in range(per_lane)
                ]
                for j in range(per_lane):
                    merged = None
                    for k in range(per_lane):
                        moved = pltpu.roll(tiles[k], ((k - j) * LOW) % LANES, 1) if k != j else tiles[k]
                        merged = moved if merged is None else jnp.where(lane_group == k, moved, merged)
                    wide[pl.ds((c * per_lane + j) * upper_p, upper_p), pl.ds(a * LANES, LANES)] = merged
        source = jnp.zeros_like(row_id)
        for j in range(labels.shape[1]):
            source = source + jnp.left_shift(jnp.bitwise_and(jnp.right_shift(row_id, j), 1), labels[b, j])
        source = jnp.bitwise_and(source, LOW - 1) * upper_p + jnp.right_shift(source, LOW.bit_length() - 1)
        chosen = (col_id == source).astype(jnp.float32).astype(jnp.bfloat16)
        for out, part in zip(outs[2 * b : 2 * b + 2], split(wide[...])):
            picked = jnp.dot(chosen, part, preferred_element_type=jnp.float32)
            out[...] = (picked.T if b == 0 else picked).astype(jnp.bfloat16)


def make_branches(pieces, right, labels, place):
    stems, grps, _, u_part, p_part, bond = pieces.shape
    upper_u, upper_p = stems * u_part, grps * p_part
    rows, cols = upper_p * LOW, upper_u * LOW
    out = jax.ShapeDtypeStruct((rows, cols), jnp.bfloat16)
    return pl.pallas_call(
        functools.partial(branch_kernel, stems, grps),
        out_shape=[jax.ShapeDtypeStruct((cols, rows), jnp.bfloat16)] * 2 + [out] * 2,
        in_specs=[pl.BlockSpec(memory_space=pltpu.SMEM)] * 2 + [pl.BlockSpec(memory_space=pltpu.VMEM)] * 2,
        out_specs=[pl.BlockSpec(memory_space=pltpu.VMEM)] * 4,
        scratch_shapes=[
            pltpu.VMEM((upper_u * upper_p, bond), jnp.float32),
            pltpu.VMEM((upper_u * upper_p, right.shape[2]), jnp.float32),
            pltpu.VMEM((rows, cols), jnp.float32),
        ],
        name="branches",
    )(place, labels, pieces, right)


def stem_kernel(stems, grps, blocks, one_high, one_low, two_high, two_low, out):
    inner = blocks.shape[2]
    x = blocks[...].reshape(stems, grps, blocks.shape[1], inner)
    slab = jnp.concatenate([x[:, g].reshape(-1, inner) for g in range(grps)], axis=1)
    turned = dot3((one_high[...], one_low[...]), split(slab), ((1,), (1,)))
    out[...] = dot3(split(turned), (two_high[...], two_low[...]), ((1,), (0,)))


def contract(blocks, parts, stems, grps):
    if blocks.shape[2] % LANES:
        x = blocks.reshape(stems, grps, *blocks.shape[1:])
        blocks = x.transpose(0, 2, 1, 3).reshape(stems, blocks.shape[1], -1)
        grps = 1
    shape = (parts[0].shape[0], parts[2].shape[1])
    return pl.pallas_call(
        functools.partial(stem_kernel, stems, grps),
        out_shape=jax.ShapeDtypeStruct(shape, jnp.float32),
        in_specs=[pl.BlockSpec(memory_space=pltpu.VMEM)] * 5,
        out_specs=pl.BlockSpec(memory_space=pltpu.VMEM),
        name="contract",
    )(blocks, *parts)


def on_device(stem_tensor, left_factors, right_factors, index_labels):
    stems, grps = lax.axis_size("stem"), lax.axis_size("grp")
    s, g = lax.axis_index("stem"), lax.axis_index("grp")
    branches, p_part, upper, bond = left_factors.shape
    u_part = upper // stems
    own = lax.dynamic_slice_in_dim(left_factors, s * u_part, u_part, axis=2)
    own = own.transpose(0, 2, 1, 3).reshape(-1, bond)
    near = [own] + [lax.ppermute(own, "grp", [(j, j ^ k) for j in range(grps)]) for k in range(1, grps)]
    blocks = lax.all_to_all(stem_tensor, ("stem", "grp"), split_axis=0, concat_axis=0, tiled=True)
    column = jnp.concatenate(near, axis=0)
    plane = [column] + [lax.ppermute(column, "stem", [(j, j ^ k) for j in range(stems)]) for k in range(2, stems, 2)]
    half = jnp.stack(plane)
    other = lax.ppermute(half, "stem", [(j, j ^ 1) for j in range(stems)])
    pieces = jnp.stack([half, other], axis=1).reshape(stems, grps, branches, u_part, p_part, bond)
    place = jnp.stack([s, g]).astype(jnp.int32)
    parts = make_branches(pieces, right_factors, index_labels, place)
    count = stem_tensor.shape[0] // (stems * grps)
    blocks = blocks.reshape(stems * grps, count, *stem_tensor.shape[1:])
    return jnp.stack([contract(blocks[:, o], parts, stems, grps) for o in range(count)])


def solution(mesh):
    placed = (P(None, "stem", "grp"), P(None, "grp", None, None), P(), P())
    return jax.shard_map(
        on_device,
        mesh=mesh,
        in_specs=placed,
        out_specs=P(("stem", "grp"), None, None),
        check_vma=False,
    )
```

time: 92.3 us -> 57.3 us (0.62)
  blocking collectives: 33.1 us -> 0 us
  waiting for transfers between devices: 0.01 us -> 27.7 us
  local copies, waits for them, and re-layouts: 23.1 us -> 1.99 us
  matrix products: 13.9 us -> 0 us
  Pallas kernels: 0 us -> 11.2 us
  other arithmetic: 11.3 us -> 0.68 us
  starting transfers between devices: 10.2 us -> 15.4 us
    all_gather x1 -> x0, blocking collectives: 33.1 us -> none  [on_device(): whole_left = lax.all_gather(left_factors, 'grp', axis=1, tiled=True)]
    ppermute x0 -> x7, waiting for transfers between devices: none -> 27.7 us  [the longest x3 23.1 us: on_device(): lax.ppermute(own, 'grp', [(j, j ^ k) for j in range(grps)])]
    dot_general x4 -> x0, matrix products: 13.9 us -> none  [the longest x2 7.84 us: assemble(): jnp.einsum('abk,kcd->acbd', left, table, precision=lax.Precision.HIGHEST)]
    and x2 -> x0, other arithmetic: 11.3 us -> none  [relabel(): return jnp.take(branch, source_rows, axis=0)]
    pallas_call x0 -> x2, Pallas kernels: none -> 11.2 us  [the longest x1 6.54 us: make_branches(): pl.pallas_call(functools.partial(branch_kernel, stems, grps), out_shape=[...]
    ppermute x0 -> x7, starting transfers between devices: none -> 8.08 us  [the longest x3 4.45 us: on_device(): lax.ppermute(own, 'grp', [(j, j ^ k) for j in range(grps)])]
    another operation x2 -> x1, local copies, waits for them, and re-layouts: 7.1 us -> 0.04 us  [on_device(): jnp.stack([half, other], axis=1)]
    transpose x2, local copies, waits for them, and re-layouts: 4.82 us -> 0.02 us  [on_device(): own = own.transpose(0, 2, 1, 3).reshape(-1, bond)]
  transfers between devices with their start and end apart: 2 -> 8, of which waited for: 0 -> 6; matrix products, arithmetic and copies ran while one was open for 42% -> 3% of each run, Pallas kernels for 0% -> 11%
where the time goes in v1:
time: 57.3 us; the launch traced here: 57 us
  waiting for transfers between devices  27.7 us (48%)
  starting transfers between devices  15.4 us (27%)
  Pallas kernels  11.2 us (20%)
  local copies, waits for them, and re-layouts  1.99 us (3%)
  other arithmetic  0.68 us (1%)
    ppermute x3, waiting for transfers between devices, on_device(): lax.ppermute(own, 'grp', [(j, j ^ k) for j in range(grps)])  23.1 us
    all_to_all x1, starting transfers between devices, on_device(): lax.all_to_all(stem_tensor, ('stem', 'grp'), split_axis=0, concat_axis=0,...  7.33 us
    pallas_call x1, Pallas kernels, make_branches(): pl.pallas_call(functools.partial(branch_kernel, stems, grps), out_shape=[...  6.54 us
    pallas_call x1, Pallas kernels, contract(): pl.pallas_call(functools.partial(stem_kernel, stems, grps), out_shape=jax...  4.62 us
    ppermute x3, starting transfers between devices, on_device(): lax.ppermute(own, 'grp', [(j, j ^ k) for j in range(grps)])  4.45 us
    ppermute x3, waiting for transfers between devices, on_device(): lax.ppermute(column, 'stem', [(j, j ^ k) for j in range(stems)])  3.7 us
    ppermute x3, starting transfers between devices, on_device(): lax.ppermute(column, 'stem', [(j, j ^ k) for j in range(stems)])  3.55 us
  transfers between devices with their start and end apart: 8, of which 6 were waited for; matrix products, arithmetic and copies ran while one was open for 3% of the time, Pallas kernels for 11%

profile of v1, /device:TPU:0, one launch (start us, length us, event | category | flops | bytes accessed | tf_op | source)
XLA Modules:
  0.0 57.0 jit_solution(10382286795769991108)
XLA Ops:
  0.0 0.0 copy-start
  0.0 7.3 %all-to-all-start = ((f32[32,64,128]{2,1,0:T(8,128)}), f32[32,64,128]{2,1,0:T(8,128)S(1)}, u32[]{:S(2)}, u32[]{:S(2)}) async-start(f32[32,64,128]{2,1,0:T(8,128)} %param.4), calls=%async_computation | async-start | bytes 2097152 | tf_op jit(solution)/shard_map/all_to_all | solution.py:118
  7.3 0.0 copy-done
  7.4 3.7 %collective-permute-start.2 = (f32[16,256]{1,0:T(8,128)S(1)}, f32[16,256]{1,0:T(8,128)S(1)}, u32[]{:S(2)}, u32[]{:S(2)}) collective-permute-start(f32[16,256]{1,0:T(8,128)S(1)} %reshape.6), channel_id=1, source_target_pairs={{0,3},{1,2},{2,1},{3,0},{4,7},{5,6},{6,5},{7,4},{8,11},{9,10},{10,... | collective-permute-start | bytes 49160 | tf_op jit(solution)/shard_map/ppermute | solution.py:117
  11.1 0.0 collective-permute-start.1
  11.1 0.8 %collective-permute-start = (f32[16,256]{1,0:T(8,128)S(1)}, f32[16,256]{1,0:T(8,128)S(1)}, u32[]{:S(2)}, u32[]{:S(2)}) collective-permute-start(f32[16,256]{1,0:T(8,128)S(1)} %reshape.6), channel_id=1, source_target_pairs={{0,1},{1,0},{2,3},{3,2},{4,5},{5,4},{6,7},{7,6},{8,9},{9,8},{10,11... | collective-permute-start | bytes 49160 | tf_op jit(solution)/shard_map/ppermute | solution.py:117
  11.9 14.2 %collective-permute-done = f32[16,256]{1,0:T(8,128)S(1)} collective-permute-done((f32[16,256]{1,0:T(8,128)S(1)}, f32[16,256]{1,0:T(8,128)S(1)}, u32[]{:S(2)}, u32[]{:S(2)}) %collective-permute-start) | collective-permute-done | bytes 16416 | tf_op jit(solution)/shard_map/ppermute | solution.py:117
  26.0 8.9 %collective-permute-done.1 = f32[16,256]{1,0:T(8,128)S(1)} collective-permute-done((f32[16,256]{1,0:T(8,128)S(1)}, f32[16,256]{1,0:T(8,128)S(1)}, u32[]{:S(2)}, u32[]{:S(2)}) %collective-permute-start.1) | collective-permute-done | bytes 16416 | tf_op jit(solution)/shard_map/ppermute | solution.py:117
  34.9 0.0 collective-permute-done.2
  35.0 2.5 %collective-permute-start.5 = (f32[64,256]{1,0:T(8,128)S(1)}, f32[64,256]{1,0:T(8,128)S(1)}, u32[]{:S(2)}, u32[]{:S(2)}) collective-permute-start(f32[64,256]{1,0:T(8,128)S(1)} %constant_dynamic-update-slice_fusion), channel_id=1, source_target_pairs={{0,24},{4,28},{8,16},{12,20},{16,8},{20,12},{24,0},{28,4},{1,25},{... | collective-permute-start | bytes 196616 | tf_op jit(solution)/shard_map/ppermute | solution.py:120
  37.4 0.5 collective-permute-start.4
  38.0 0.6 collective-permute-start.3
  38.5 1.8 %collective-permute-done.5 = f32[64,256]{1,0:T(8,128)S(1)} collective-permute-done((f32[64,256]{1,0:T(8,128)S(1)}, f32[64,256]{1,0:T(8,128)S(1)}, u32[]{:S(2)}, u32[]{:S(2)}) %collective-permute-start.5) | collective-permute-done | bytes 65568 | tf_op jit(solution)/shard_map/ppermute | solution.py:120
  40.3 1.4 %collective-permute-done.4 = f32[64,256]{1,0:T(8,128)S(1)} collective-permute-done((f32[64,256]{1,0:T(8,128)S(1)}, f32[64,256]{1,0:T(8,128)S(1)}, u32[]{:S(2)}, u32[]{:S(2)}) %collective-permute-start.4) | collective-permute-done | bytes 65568 | tf_op jit(solution)/shard_map/ppermute | solution.py:120
  41.7 0.5 collective-permute-done.3
  42.3 0.1 collective-permute-start.6
  42.3 0.6 %pad_add_fusion.place = s32[2]{0:T(128)} fusion(s32[1]{0:T(128)} %bitcast.1, s32[1]{0:T(128)} %bitcast), kind=kLoop, calls=%fused_computation.7 | loop fusion | flops 2 | bytes 16 | tf_op jit(solution)/shard_map/stack | solution.py:124
  43.0 0.9 %collective-permute-done.6 = f32[4,64,256]{2,1,0:T(8,128)S(1)} collective-permute-done((f32[4,64,256]{2,1,0:T(8,128)S(1)}, f32[4,64,256]{2,1,0:T(8,128)S(1)}, u32[]{:S(2)}, u32[]{:S(2)}) %collective-permute-start.6) | collective-permute-done | bytes 262176 | tf_op jit(solution)/shard_map/ppermute | solution.py:122
  43.9 0.9 %reshape.7.pieces = f32[8,4,2,2,4,256]{5,4,3,2,1,0:T(4,128)} reshape(f32[4,2,64,256]{3,2,1,0:T(8,128)S(1)} %copy.7) | data formatting | bytes 1048576 | tf_op jit(solution)/shard_map/reshape | solution.py:123
  44.9 6.5 %branches.1 = (bf16[512,512]{1,0:T(8,128)(2,1)}, bf16[512,512]{1,0:T(8,128)(2,1)}, bf16[512,512]{1,0:T(8,128)(2,1)}, bf16[512,512]{1,0:T(8,128)(2,1)}) custom-call(s32[2]{0:T(128)} %pad_add_fusion.place, s32[2,9]{1,0:T(2,128)} %labels.1, f32[8,4,2,2,4,256]{5,4,3,2,1,0:T(4,128)} %reshape.7.pieces, f32[2,256,1024]{2,1,0:T(8,128)} %right.1), custom_call_target="tpu_custom_call" | custom-call | tf_op jit(solution)/shard_map/branches/pallas_call | solution.py:73
  51.4 0.0 all-to-all-done.blocks
  51.4 0.0 copy-start.1
  51.4 1.0 %copy-done.1 = f32[32,64,128]{2,1,0:T(8,128)} copy-done((f32[32,64,128]{2,1,0:T(8,128)}, f32[32,64,128]{2,1,0:T(8,128)S(1)}, u32[]{:S(2)}) %copy-start.1) | copy-done | bytes 1048600
  52.4 4.6 %contract.1 = f32[512,512]{1,0:T(8,128)} custom-call(f32[32,64,128]{2,1,0:T(8,128)} %copy-done.1, bf16[512,512]{1,0:T(8,128)(2,1)} %get-tuple-element.9.one_high, bf16[512,512]{1,0:T(8,128)(2,1)} %get-tuple-element.10.one_low, bf16[512,512]{1,0:T(8,128)(2,1)} %get-tuple-element.11.two_high, bf16[512,512]{1,0:T(8,128)(2,1)} %get-tuple-element.12.two_low), custom_call_target="tpu_custom_call" | custom-call | tf_op jit(solution)/shard_map/contract/pallas_call | solution.py:101
  (10 shorter events, 0.1 us)
Async XLA Ops:
  0.0 7.3 %copy-start = (f32[2,4,16,256]{3,2,1,0:T(8,128)S(1)}, f32[2,4,16,256]{3,2,1,0:T(8,128)}, u32[]{:S(2)}) copy-start(f32[2,4,16,256]{3,2,1,0:T(8,128)} %param.5) | copy-start | bytes 393220
  0.0 51.4 %all-to-all-start = ((f32[32,64,128]{2,1,0:T(8,128)}), f32[32,64,128]{2,1,0:T(8,128)S(1)}, u32[]{:S(2)}, u32[]{:S(2)}) async-start(f32[32,64,128]{2,1,0:T(8,128)} %param.4), calls=%async_computation | async-start | bytes 2097152 | tf_op jit(solution)/shard_map/all_to_all | solution.py:118
  7.4 27.5 %collective-permute-start.2 = (f32[16,256]{1,0:T(8,128)S(1)}, f32[16,256]{1,0:T(8,128)S(1)}, u32[]{:S(2)}, u32[]{:S(2)}) collective-permute-start(f32[16,256]{1,0:T(8,128)S(1)} %reshape.6), channel_id=1, source_target_pairs={{0,3},{1,2},{2,1},{3,0},{4,7},{5,6},{6,5},{7,4},{8,11},{9,10},{10,... | collective-permute-start | bytes 49160 | tf_op jit(solution)/shard_map/ppermute | solution.py:117
  11.1 23.9 %collective-permute-start.1 = (f32[16,256]{1,0:T(8,128)S(1)}, f32[16,256]{1,0:T(8,128)S(1)}, u32[]{:S(2)}, u32[]{:S(2)}) collective-permute-start(f32[16,256]{1,0:T(8,128)S(1)} %reshape.6), channel_id=1, source_target_pairs={{0,2},{1,3},{2,0},{3,1},{4,6},{5,7},{6,4},{7,5},{8,10},{9,11},{10,... | collective-permute-start | bytes 49160 | tf_op jit(solution)/shard_map/ppermute | solution.py:117
  11.1 14.9 %collective-permute-start = (f32[16,256]{1,0:T(8,128)S(1)}, f32[16,256]{1,0:T(8,128)S(1)}, u32[]{:S(2)}, u32[]{:S(2)}) collective-permute-start(f32[16,256]{1,0:T(8,128)S(1)} %reshape.6), channel_id=1, source_target_pairs={{0,1},{1,0},{2,3},{3,2},{4,5},{5,4},{6,7},{7,6},{8,9},{9,8},{10,11... | collective-permute-start | bytes 49160 | tf_op jit(solution)/shard_map/ppermute | solution.py:117
  35.0 5.3 %collective-permute-start.5 = (f32[64,256]{1,0:T(8,128)S(1)}, f32[64,256]{1,0:T(8,128)S(1)}, u32[]{:S(2)}, u32[]{:S(2)}) collective-permute-start(f32[64,256]{1,0:T(8,128)S(1)} %constant_dynamic-update-slice_fusion), channel_id=1, source_target_pairs={{0,24},{4,28},{8,16},{12,20},{16,8},{20,12},{24,0},{28,4},{1,25},{... | collective-permute-start | bytes 196616 | tf_op jit(solution)/shard_map/ppermute | solution.py:120
  37.4 4.3 %collective-permute-start.4 = (f32[64,256]{1,0:T(8,128)S(1)}, f32[64,256]{1,0:T(8,128)S(1)}, u32[]{:S(2)}, u32[]{:S(2)}) collective-permute-start(f32[64,256]{1,0:T(8,128)S(1)} %constant_dynamic-update-slice_fusion), channel_id=1, source_target_pairs={{0,16},{4,20},{8,24},{12,28},{16,0},{20,4},{24,8},{28,12},{1,17},{... | collective-permute-start | bytes 196616 | tf_op jit(solution)/shard_map/ppermute | solution.py:120
  38.0 4.3 %collective-permute-start.3 = (f32[64,256]{1,0:T(8,128)S(1)}, f32[64,256]{1,0:T(8,128)S(1)}, u32[]{:S(2)}, u32[]{:S(2)}) collective-permute-start(f32[64,256]{1,0:T(8,128)S(1)} %constant_dynamic-update-slice_fusion), channel_id=1, source_target_pairs={{0,8},{4,12},{8,0},{12,4},{16,24},{20,28},{24,16},{28,20},{1,9},{5... | collective-permute-start | bytes 196616 | tf_op jit(solution)/shard_map/ppermute | solution.py:120
  42.3 1.6 %collective-permute-start.6 = (f32[4,64,256]{2,1,0:T(8,128)S(1)}, f32[4,64,256]{2,1,0:T(8,128)S(1)}, u32[]{:S(2)}, u32[]{:S(2)}) collective-permute-start(f32[4,64,256]{2,1,0:T(8,128)S(1)} %get-tuple-element.14), channel_id=1, source_target_pairs={{0,4},{4,0},{8,12},{12,8},{16,20},{20,16},{24,28},{28,24},{1,5},{5... | collective-permute-start | bytes 786440 | tf_op jit(solution)/shard_map/ppermute | solution.py:122
  51.4 1.0 %copy-start.1 = (f32[32,64,128]{2,1,0:T(8,128)}, f32[32,64,128]{2,1,0:T(8,128)S(1)}, u32[]{:S(2)}) copy-start(f32[32,64,128]{2,1,0:T(8,128)S(1)} %all-to-all-done.blocks) | copy-start | bytes 3145732

commit v2 on v1

v2 whole, which is shorter than its diff:
```python
import functools
import jax
import jax.numpy as jnp
from jax import lax
from jax.experimental import pallas as pl
from jax.experimental.pallas import tpu as pltpu
from jax.sharding import PartitionSpec as P


LOW = 32
LANES = 128
LIMIT = 20 * 2**20
VMEM = pl.BlockSpec(memory_space=pltpu.VMEM)
AWAY = pl.BlockSpec(memory_space=pl.ANY)
SMEM = pl.BlockSpec(memory_space=pltpu.SMEM)


def on_chip(x):
    return pltpu.with_memory_space_constraint(x, pltpu.VMEM)


def off_chip(x):
    return pltpu.with_memory_space_constraint(x, pltpu.HBM)


def split(x):
    high = x.astype(jnp.bfloat16)
    low = (x - high.astype(jnp.float32)).astype(jnp.bfloat16)
    return high, low


def dot3(a, b, dims):
    (a_high, a_low), (b_high, b_low) = a, b

    def one(x, y):
        return lax.dot_general(x, y, (dims, ((), ())), preferred_element_type=jnp.float32)

    return one(a_high, b_high) + (one(a_high, b_low) + one(a_low, b_high))


def order_rows(place, own, near, same, other, ordered, b):
    _, p_part, upper, _ = own.shape
    chips = same.shape[0]
    core, chip = jnp.bitwise_and(place[0], 1), jnp.right_shift(place[0], 1)
    far = upper // chips
    per_u = 4 * p_part
    for n, ref in enumerate((own, near)):
        for p in range(p_part):
            rows = ref[b, p]
            for u in range(upper):
                ordered[pl.ds(u * per_u + n * p_part + p, 1), :] = rows[u : u + 1]
    for c in range(chips):
        for e in range(2):
            fetched = jnp.where(core == e, same[chip ^ c], other[chip ^ c])
            for u in range(far):
                at = (c * far + u) * per_u + (2 + e) * p_part
                ordered[pl.ds(at, p_part), :] = fetched[(b * far + u) * p_part :][:p_part]


def branch_kernel(fetched, place, labels, *refs):
    ordered_refs, refs = refs[: 4 if fetched else 1], refs[4 if fetched else 1 :]
    right_away, one_high, one_low, two, ordered, product, wide, right, arrived = refs
    brings = [pltpu.make_async_copy(right_away.at[b], right.at[b], arrived.at[b]) for b in range(right.shape[0])]
    for bring in brings:
        bring.start()
    branches = right.shape[0]
    rows, cols = wide.shape
    upper_p = rows // LOW
    per_lane = LANES // LOW
    lane_group = lax.broadcasted_iota(jnp.int32, (upper_p, LANES), 1) // LOW
    row_id = lax.broadcasted_iota(jnp.int32, (rows, 1), 0)
    col_id = lax.broadcasted_iota(jnp.int32, (rows, rows), 1)
    for b in range(branches):
        if fetched:
            order_rows(place, *ordered_refs, ordered, b)
        else:
            ordered[...] = ordered_refs[0][b]
        brings[b].wait()
        product[...] = dot3(split(ordered[...]), split(right[b]), ((1,), (0,)))
        for c in range(LOW * LOW // LANES):
            for a in range(cols // LANES):
                tiles = [
                    product[pl.ds((a * per_lane + k) * upper_p, upper_p), pl.ds(c * LANES, LANES)]
                    for k in range(per_lane)
                ]
                for j in range(per_lane):
                    merged = None
                    for k in range(per_lane):
                        moved = pltpu.roll(tiles[k], ((k - j) * LOW) % LANES, 1) if k != j else tiles[k]
                        merged = moved if merged is None else jnp.where(lane_group == k, moved, merged)
                    wide[pl.ds((c * per_lane + j) * upper_p, upper_p), pl.ds(a * LANES, LANES)] = merged
        source = jnp.zeros_like(row_id)
        for j in range(labels.shape[1]):
            source = source + jnp.left_shift(jnp.bitwise_and(jnp.right_shift(row_id, j), 1), labels[b, j])
        upper = jnp.bitwise_xor(jnp.right_shift(source, LOW.bit_length() - 1), place[1])
        source = jnp.bitwise_and(source, LOW - 1) * upper_p + upper
        chosen = (col_id == source).astype(jnp.float32).astype(jnp.bfloat16)
        for n, part in enumerate(split(wide[...])):
            picked = jnp.dot(chosen, part, preferred_element_type=jnp.float32)
            if b == 0:
                (one_high, one_low)[n][...] = picked.T.astype(jnp.bfloat16)
            else:
                two[n] = picked.astype(jnp.bfloat16)


def make_branches(firsts, right, labels, place, rows, cols):
    branches, bond, low_pairs = right.shape
    fetched = len(firsts) > 1
    return pl.pallas_call(
        functools.partial(branch_kernel, fetched),
        out_shape=[pltpu.VMEM((cols, rows), jnp.bfloat16)] * 2 + [pltpu.HBM((2, rows, cols), jnp.bfloat16)],
        in_specs=[SMEM, SMEM] + [VMEM] * len(firsts) + [AWAY],
        out_specs=[VMEM] * 3,
        scratch_shapes=[
            pltpu.VMEM((rows * cols // (LOW * LOW), bond), jnp.float32),
            pltpu.VMEM((rows * cols // (LOW * LOW), low_pairs), jnp.float32),
            pltpu.VMEM((rows, cols), jnp.float32),
            pltpu.VMEM(right.shape, right.dtype),
            pltpu.SemaphoreType.DMA((branches,)),
        ],
        compiler_params=pltpu.CompilerParams(vmem_limit_bytes=LIMIT),
        name="branches",
    )(place, labels, *(on_chip(x) for x in firsts), off_chip(right))


def stem_kernel(stems, grps, steps, blocks, one_high, one_low, two_away, out_away, two, out, arrived, left):
    bring = pltpu.make_async_copy(two_away, two, arrived)
    bring.start()
    inner = blocks.shape[2]
    x = blocks[...].reshape(stems, grps, blocks.shape[1], inner)
    slab = jnp.concatenate([x[:, g].reshape(-1, inner) for g in range(grps)], axis=1)
    turned = split(dot3((one_high[...], one_low[...]), split(slab), ((1,), (1,))))
    bring.wait()
    sends, start = [], 0
    for n, size in enumerate(steps):
        rows = pl.ds(start, size)
        out[rows, :] = dot3(
            tuple(t[start : start + size] for t in turned), (two[0], two[1]), ((1,), (0,))
        )
        sends.append(pltpu.make_async_copy(out.at[rows], out_away.at[rows], left.at[n]))
        sends[-1].start()
        start += size
    for send in sends:
        send.wait()


def contract(blocks, parts, stems, grps):
    if blocks.shape[2] % LANES:
        x = blocks.reshape(stems, grps, *blocks.shape[1:])
        blocks = x.transpose(0, 2, 1, 3).reshape(stems, blocks.shape[1], -1)
        grps = 1
    one_high, one_low, two = parts
    shape = (one_high.shape[0], two.shape[2])
    steps = (shape[0] // 2, shape[0] // 4, shape[0] // 4)
    return pl.pallas_call(
        functools.partial(stem_kernel, stems, grps, steps),
        out_shape=jax.ShapeDtypeStruct(shape, jnp.float32),
        in_specs=[VMEM] * 3 + [AWAY],
        out_specs=AWAY,
        scratch_shapes=[
            pltpu.VMEM(two.shape, two.dtype),
            pltpu.VMEM(shape, jnp.float32),
            pltpu.SemaphoreType.DMA,
            pltpu.SemaphoreType.DMA((len(steps),)),
        ],
        compiler_params=pltpu.CompilerParams(vmem_limit_bytes=LIMIT),
        name="contract",
    )(on_chip(blocks), on_chip(one_high), on_chip(one_low), off_chip(two))


def fetch(left, stems, grps, s):
    _, _, upper, bond = left.shape
    far = 2 * upper // stems
    near = lax.ppermute(left, "grp", [(j, j ^ 1) for j in range(grps)])
    part = lax.dynamic_slice_in_dim(left, (s // 2) * far, far, axis=2).transpose(0, 2, 1, 3).reshape(-1, bond)
    pairs = [(i * grps + j, i * grps + (j ^ (2 + i % 2))) for i in range(stems) for j in range(grps)]
    column = lax.ppermute(part, ("stem", "grp"), pairs)
    plane = [column] + [lax.ppermute(column, "stem", [(j, j ^ k) for j in range(stems)]) for k in range(2, stems, 2)]
    same = jnp.stack(plane)
    other = lax.ppermute(same, "stem", [(j, j ^ 1) for j in range(stems)])
    return left, near, same, other


def on_device(stem_tensor, left_factors, right_factors, index_labels):
    stems, grps = lax.axis_size("stem"), lax.axis_size("grp")
    s, g = lax.axis_index("stem"), lax.axis_index("grp")
    branches, p_part, upper, bond = left_factors.shape
    rows, cols = p_part * grps * LOW, upper * LOW
    if grps == 4:
        firsts, cross = fetch(left_factors, stems, grps, s), g * p_part
    else:
        whole = lax.all_gather(left_factors, "grp", axis=1, tiled=True)
        firsts, cross = (whole.transpose(0, 2, 1, 3).reshape(branches, -1, bond),), 0 * g
    blocks = lax.all_to_all(stem_tensor, ("stem", "grp"), split_axis=0, concat_axis=0, tiled=True)
    place = jnp.stack([s, cross]).astype(jnp.int32)
    parts = make_branches(firsts, right_factors, index_labels, place, rows, cols)
    count = stem_tensor.shape[0] // (stems * grps)
    blocks = blocks.reshape(stems * grps, count, *stem_tensor.shape[1:])
    return jnp.stack([contract(blocks[:, o], parts, stems, grps) for o in range(count)])


def solution(mesh):
    placed = (P(None, "stem", "grp"), P(None, "grp", None, None), P(), P())
    return jax.shard_map(
        on_device,
        mesh=mesh,
        in_specs=placed,
        out_specs=P(("stem", "grp"), None, None),
        check_vma=False,
    )
```

time: 57.3 us -> 54.3 us (0.948)
  local copies, waits for them, and re-layouts: 1.99 us -> 0.05 us
  waiting for transfers between devices: 27.7 us -> 29.6 us
  starting transfers between devices: 15.4 us -> 13.6 us
  other arithmetic: 0.68 us -> 0.08 us
  Pallas kernels: 11.2 us -> 10.6 us
    ppermute x7 -> x6, waiting for transfers between devices: 27.7 us -> 29.6 us  [the longest x1 24.8 us: fetch(): column = lax.ppermute(part, ('stem', 'grp'), pairs)]
    ppermute x7 -> x6, starting transfers between devices: 8.08 us -> 6.3 us  [the longest x3 3.49 us: fetch(): lax.ppermute(column, 'stem', [(j, j ^ k) for j in range(stems)])]
    unnamed x7 -> x4, local copies, waits for them, and re-layouts: 0.98 us -> 0.01 us
    reshape x2 -> x1, local copies, waits for them, and re-layouts: 0.95 us -> 0.02 us  [fetch(): lax.dynamic_slice_in_dim(left, s // 2 * far, far, axis=2)]
    another operation x3 -> x2, other arithmetic: 0.68 us -> 0.08 us  [the longest x1 0.08 us: on_device(): place = jnp.stack([s, cross]).astype(jnp.int32)]
  transfers between devices with their start and end apart: 8 -> 7, of which waited for: 6 -> 5; matrix products, arithmetic and copies ran while one was open for 3% -> 0% of each run, Pallas kernels for 11% -> 13%
where the time goes in v2:
time: 54.3 us; the launch traced here: 54.1 us
  waiting for transfers between devices  29.6 us (55%)
  starting transfers between devices  13.6 us (25%)
  Pallas kernels  10.6 us (20%)
    ppermute x1, waiting for transfers between devices, fetch(): column = lax.ppermute(part, ('stem', 'grp'), pairs)  24.8 us
    all_to_all x1, starting transfers between devices, on_device(): lax.all_to_all(stem_tensor, ('stem', 'grp'), split_axis=0, concat_axis=0,...  7.33 us
    pallas_call x1, Pallas kernels, make_branches(): pl.pallas_call(functools.partial(branch_kernel, fetched), out_shape=[pltp...  6.99 us
    pallas_call x1, Pallas kernels, contract(): pl.pallas_call(functools.partial(stem_kernel, stems, grps, steps), out_sh...  3.64 us
    ppermute x3, starting transfers between devices, fetch(): lax.ppermute(column, 'stem', [(j, j ^ k) for j in range(stems)])  3.49 us
    ppermute x3, waiting for transfers between devices, fetch(): lax.ppermute(column, 'stem', [(j, j ^ k) for j in range(stems)])  3.35 us
    ppermute x1, starting transfers between devices, fetch(): column = lax.ppermute(part, ('stem', 'grp'), pairs)  2.74 us
    ppermute x1, waiting for transfers between devices, fetch(): near = lax.ppermute(left, 'grp', [(j, j ^ 1) for j in range(grps)])  1.44 us
  transfers between devices with their start and end apart: 7, of which 5 were waited for; matrix products, arithmetic and copies ran while one was open for 0% of the time, Pallas kernels for 13%

profile of v2, /device:TPU:0, one launch (start us, length us, event | category | flops | bytes accessed | tf_op | source)
XLA Modules:
  0.0 54.1 jit_solution(8021911085334016103)
XLA Ops:
  0.0 0.0 copy-start
  0.0 0.0 copy-start.1
  0.0 7.3 %all-to-all-start = ((f32[32,64,128]{2,1,0:T(8,128)}), f32[32,64,128]{2,1,0:T(8,128)S(1)}, u32[]{:S(2)}, u32[]{:S(2)}) async-start(f32[32,64,128]{2,1,0:T(8,128)} %param.4), calls=%async_computation | async-start | bytes 2097152 | tf_op jit(solution)/shard_map/all_to_all | solution.py:194
  7.4 0.0 copy-done
  7.4 2.7 %collective-permute-start.1 = (f32[32,256]{1,0:T(8,128)S(1)}, f32[32,256]{1,0:T(8,128)S(1)}, u32[]{:S(2)}, u32[]{:S(2)}) collective-permute-start(f32[32,256]{1,0:T(8,128)S(1)} %reshape.3), channel_id=1, source_target_pairs={{0,2},{1,3},{2,0},{3,1},{4,7},{5,6},{6,5},{7,4},{8,10},{9,11},{10,... | collective-permute-start | bytes 98312 | tf_op jit(solution)/shard_map/ppermute | solution.py:177
  10.2 24.8 %collective-permute-done.1 = f32[32,256]{1,0:T(8,128)S(1)} collective-permute-done((f32[32,256]{1,0:T(8,128)S(1)}, f32[32,256]{1,0:T(8,128)S(1)}, u32[]{:S(2)}, u32[]{:S(2)}) %collective-permute-start.1) | collective-permute-done | bytes 32800 | tf_op jit(solution)/shard_map/ppermute | solution.py:177
  34.9 2.4 %collective-permute-start.4 = (f32[32,256]{1,0:T(8,128)S(1)}, f32[32,256]{1,0:T(8,128)S(1)}, u32[]{:S(2)}, u32[]{:S(2)}) collective-permute-start(f32[32,256]{1,0:T(8,128)S(1)} %collective-permute-done.1), channel_id=1, source_target_pairs={{0,24},{4,28},{8,16},{12,20},{16,8},{20,12},{24,0},{28,4},{1,25},{... | collective-permute-start | bytes 98312 | tf_op jit(solution)/shard_map/ppermute | solution.py:178
  37.3 0.5 collective-permute-start.3
  37.9 0.6 %collective-permute-start.2 = (f32[32,256]{1,0:T(8,128)S(1)}, f32[32,256]{1,0:T(8,128)S(1)}, u32[]{:S(2)}, u32[]{:S(2)}) collective-permute-start(f32[32,256]{1,0:T(8,128)S(1)} %collective-permute-done.1), channel_id=1, source_target_pairs={{0,8},{4,12},{8,0},{12,4},{16,24},{20,28},{24,16},{28,20},{1,9},{5... | collective-permute-start | bytes 98312 | tf_op jit(solution)/shard_map/ppermute | solution.py:178
  38.4 0.0 collective-permute-start
  38.4 1.3 %collective-permute-done.4 = f32[32,256]{1,0:T(8,128)S(1)} collective-permute-done((f32[32,256]{1,0:T(8,128)S(1)}, f32[32,256]{1,0:T(8,128)S(1)}, u32[]{:S(2)}, u32[]{:S(2)}) %collective-permute-start.4) | collective-permute-done | bytes 32800 | tf_op jit(solution)/shard_map/ppermute | solution.py:178
  39.8 1.5 %collective-permute-done.3 = f32[32,256]{1,0:T(8,128)S(1)} collective-permute-done((f32[32,256]{1,0:T(8,128)S(1)}, f32[32,256]{1,0:T(8,128)S(1)}, u32[]{:S(2)}, u32[]{:S(2)}) %collective-permute-start.3) | collective-permute-done | bytes 32800 | tf_op jit(solution)/shard_map/ppermute | solution.py:178
  41.3 0.5 collective-permute-done.2
  41.8 0.1 collective-permute-start.5
  41.9 0.1 pad_add_fusion.place
  42.0 1.4 %collective-permute-done.refs_1_ = f32[2,4,16,256]{3,2,1,0:T(8,128)S(1)} collective-permute-done((f32[2,4,16,256]{3,2,1,0:T(8,128)S(1)}, f32[2,4,16,256]{3,2,1,0:T(8,128)S(1)}, u32[]{:S(2)}, u32[]{:S(2)}) %collective-permute-start) | collective-permute-done | bytes 131104 | tf_op jit(solution)/shard_map/ppermute | solution.py:174
  43.4 0.0 collective-permute-done.5.refs_3_
  43.4 0.0 copy-done.1
  43.4 7.0 %branches.1 = (bf16[512,512]{1,0:T(8,128)(2,1)S(1)}, bf16[512,512]{1,0:T(8,128)(2,1)S(1)}, bf16[2,512,512]{2,1,0:T(8,128)(2,1)}) custom-call(s32[2]{0:T(128)S(1)} %pad_add_fusion.place, s32[2,9]{1,0:T(2,128)S(1)} %copy-done.1, f32[2,4,16,256]{3,2,1,0:T(8,128)S(1)} %copy-done, f32[2,4,16,256]{3,2,1,0:T(8,128)S(1)} %collective-permute-done.refs_1_, ...), custom_call_target="tpu_custom_call" | custom-call | tf_op jit(solution)/shard_map/branches/pallas_call | solution.py:109
  50.4 0.0 all-to-all-done.blocks
  50.4 3.6 %contract.1 = f32[512,512]{1,0:T(8,128)} custom-call(f32[32,64,128]{2,1,0:T(8,128)S(1)} %all-to-all-done.blocks, bf16[512,512]{1,0:T(8,128)(2,1)S(1)} %get-tuple-element.8.one_high, bf16[512,512]{1,0:T(8,128)(2,1)S(1)} %get-tuple-element.9.one_low, bf16[2,512,512]{2,1,0:T(8,128)(2,1)} %get-tuple-element.10.two_away), custom_call_target="tpu_custom_call" | custom-call | tf_op jit(solution)/shard_map/contract/pallas_call | solution.py:155
  (4 shorter events, 0.1 us)
Async XLA Ops:
  0.0 7.4 %copy-start = (f32[2,4,16,256]{3,2,1,0:T(8,128)S(1)}, f32[2,4,16,256]{3,2,1,0:T(8,128)}, u32[]{:S(2)}) copy-start(f32[2,4,16,256]{3,2,1,0:T(8,128)} %refs_0_.1) | copy-start | bytes 393220
  0.0 43.4 %copy-start.1 = (s32[2,9]{1,0:T(2,128)S(1)}, s32[2,9]{1,0:T(2,128)}, u32[]{:S(2)}) copy-start(s32[2,9]{1,0:T(2,128)} %labels.1) | copy-start | bytes 220
  0.0 50.4 %all-to-all-start = ((f32[32,64,128]{2,1,0:T(8,128)}), f32[32,64,128]{2,1,0:T(8,128)S(1)}, u32[]{:S(2)}, u32[]{:S(2)}) async-start(f32[32,64,128]{2,1,0:T(8,128)} %param.4), calls=%async_computation | async-start | bytes 2097152 | tf_op jit(solution)/shard_map/all_to_all | solution.py:194
  7.4 27.5 %collective-permute-start.1 = (f32[32,256]{1,0:T(8,128)S(1)}, f32[32,256]{1,0:T(8,128)S(1)}, u32[]{:S(2)}, u32[]{:S(2)}) collective-permute-start(f32[32,256]{1,0:T(8,128)S(1)} %reshape.3), channel_id=1, source_target_pairs={{0,2},{1,3},{2,0},{3,1},{4,7},{5,6},{6,5},{7,4},{8,10},{9,11},{10,... | collective-permute-start | bytes 98312 | tf_op jit(solution)/shard_map/ppermute | solution.py:177
  34.9 4.8 %collective-permute-start.4 = (f32[32,256]{1,0:T(8,128)S(1)}, f32[32,256]{1,0:T(8,128)S(1)}, u32[]{:S(2)}, u32[]{:S(2)}) collective-permute-start(f32[32,256]{1,0:T(8,128)S(1)} %collective-permute-done.1), channel_id=1, source_target_pairs={{0,24},{4,28},{8,16},{12,20},{16,8},{20,12},{24,0},{28,4},{1,25},{... | collective-permute-start | bytes 98312 | tf_op jit(solution)/shard_map/ppermute | solution.py:178
  37.3 3.9 %collective-permute-start.3 = (f32[32,256]{1,0:T(8,128)S(1)}, f32[32,256]{1,0:T(8,128)S(1)}, u32[]{:S(2)}, u32[]{:S(2)}) collective-permute-start(f32[32,256]{1,0:T(8,128)S(1)} %collective-permute-done.1), channel_id=1, source_target_pairs={{0,16},{4,20},{8,24},{12,28},{16,0},{20,4},{24,8},{28,12},{1,17},{... | collective-permute-start | bytes 98312 | tf_op jit(solution)/shard_map/ppermute | solution.py:178
  37.9 3.9 %collective-permute-start.2 = (f32[32,256]{1,0:T(8,128)S(1)}, f32[32,256]{1,0:T(8,128)S(1)}, u32[]{:S(2)}, u32[]{:S(2)}) collective-permute-start(f32[32,256]{1,0:T(8,128)S(1)} %collective-permute-done.1), channel_id=1, source_target_pairs={{0,8},{4,12},{8,0},{12,4},{16,24},{20,28},{24,16},{28,20},{1,9},{5... | collective-permute-start | bytes 98312 | tf_op jit(solution)/shard_map/ppermute | solution.py:178
  38.4 5.0 %collective-permute-start = (f32[2,4,16,256]{3,2,1,0:T(8,128)S(1)}, f32[2,4,16,256]{3,2,1,0:T(8,128)S(1)}, u32[]{:S(2)}, u32[]{:S(2)}) collective-permute-start(f32[2,4,16,256]{3,2,1,0:T(8,128)S(1)} %copy-done), channel_id=1, source_target_pairs={{0,1},{1,0},{2,3},{3,2},{4,5},{5,4},{6,7},{7,6},{8,9},{9,8},{10,11... | collective-permute-start | bytes 393224 | tf_op jit(solution)/shard_map/ppermute | solution.py:174
  41.8 1.6 %collective-permute-start.5 = (f32[4,32,256]{2,1,0:T(8,128)S(1)}, f32[4,32,256]{2,1,0:T(8,128)S(1)}, u32[]{:S(2)}, u32[]{:S(2)}) collective-permute-start(f32[4,32,256]{2,1,0:T(8,128)S(1)} %pad_maximum_fusion.refs_2_), channel_id=1, source_target_pairs={{0,4},{4,0},{8,12},{12,8},{16,20},{20,16},{24,28},{28,24},{1,5},{5... | collective-permute-start | bytes 393224 | tf_op jit(solution)/shard_map/ppermute | solution.py:180

commit v3 on v2

v3 whole, which is shorter than its diff:
```python
import functools
import jax
import jax.numpy as jnp
from jax import lax
from jax.experimental import pallas as pl
from jax.experimental.pallas import tpu as pltpu
from jax.sharding import PartitionSpec as P


LOW = 32
LANES = 128
LIMIT = 20 * 2**20
VMEM = pl.BlockSpec(memory_space=pltpu.VMEM)
AWAY = pl.BlockSpec(memory_space=pl.ANY)
SMEM = pl.BlockSpec(memory_space=pltpu.SMEM)


def on_chip(x):
    return pltpu.with_memory_space_constraint(x, pltpu.VMEM)


def off_chip(x):
    return pltpu.with_memory_space_constraint(x, pltpu.HBM)


def split(x):
    high = x.astype(jnp.bfloat16)
    low = (x - high.astype(jnp.float32)).astype(jnp.bfloat16)
    return high, low


def dot3(a, b, dims):
    (a_high, a_low), (b_high, b_low) = a, b

    def one(x, y):
        return lax.dot_general(x, y, (dims, ((), ())), preferred_element_type=jnp.float32)

    return one(a_high, b_high) + (one(a_high, b_low) + one(a_low, b_high))


def order_rows(place, own, near, same, other, ordered, b):
    _, p_part, upper, _ = own.shape
    core = jnp.bitwise_and(place[0], 1)
    per_u = 4 * p_part
    for p in range(p_part):
        mine, its = same[b, p], other[b, p]
        for n, rows in enumerate((own[b, p], near[b, p], jnp.where(core == 0, mine, its), jnp.where(core == 0, its, mine))):
            for u in range(upper):
                ordered[pl.ds(u * per_u + n * p_part + p, 1), :] = rows[u : u + 1]


def regroup(tiles, lane_group):
    for bit in range(len(tiles).bit_length() - 1):
        step, shift = 1 << bit, LOW << bit
        upper = jnp.bitwise_and(jnp.right_shift(lane_group, bit), 1) == 1
        for k in range(len(tiles)):
            if k & step == 0:
                low, high = tiles[k], tiles[k | step]
                tiles[k] = jnp.where(upper, pltpu.roll(high, shift, 1), low)
                tiles[k | step] = jnp.where(upper, high, pltpu.roll(low, LANES - shift, 1))
    return tiles


def branch_kernel(fetched, place, labels, *refs):
    count = 4 if fetched else 1
    away, refs = refs[:count], refs[count:]
    right_away, one_high, one_low, two, ordered, product, wide, chosen, right, arrived = refs[:10]
    near_by, here = refs[10:-1], refs[-1]
    brings = [pltpu.make_async_copy(right_away.at[b], right.at[b], arrived.at[b]) for b in range(right.shape[0])]
    takes = [pltpu.make_async_copy(x, y, here.at[n]) for n, (x, y) in enumerate(zip(away, near_by))]
    for take in takes:
        take.start()
    brings[0].start()
    branches = right.shape[0]
    rows, cols = wide.shape
    upper_p = rows // LOW
    per_lane = LANES // LOW
    lane_group = lax.broadcasted_iota(jnp.int32, (upper_p, LANES), 1) // LOW
    to_id = lax.broadcasted_iota(jnp.int32, (1, rows), 1)
    from_id = lax.broadcasted_iota(jnp.int32, (rows, rows), 0)
    for b in range(branches):
        source = jnp.zeros_like(to_id)
        for j in range(labels.shape[1]):
            source = source + jnp.left_shift(jnp.bitwise_and(jnp.right_shift(to_id, j), 1), labels[b, j])
        upper = jnp.bitwise_xor(jnp.right_shift(source, LOW.bit_length() - 1), place[1])
        source = jnp.bitwise_and(source, LOW - 1) * upper_p + upper
        chosen[b] = (from_id == source).astype(jnp.float32).astype(jnp.bfloat16)
    for take in takes:
        take.wait()
    for b in range(branches):
        if fetched:
            order_rows(place, *near_by, ordered, b)
        else:
            ordered[...] = near_by[0][b]
        brings[b].wait()
        if b + 1 < branches:
            brings[b + 1].start()
        product[...] = dot3(split(ordered[...]), split(right[b]), ((1,), (0,)))
        for c in range(LOW * LOW // LANES):
            for a in range(cols // LANES):
                tiles = [
                    product[pl.ds((a * per_lane + k) * upper_p, upper_p), pl.ds(c * LANES, LANES)]
                    for k in range(per_lane)
                ]
                for j, tile in enumerate(regroup(tiles, lane_group)):
                    wide[pl.ds((c * per_lane + j) * upper_p, upper_p), pl.ds(a * LANES, LANES)] = tile
        for n, part in enumerate(split(wide[...])):
            sides = (part, chosen[b]) if b == 0 else (chosen[b], part)
            picked = lax.dot_general(*sides, (((0,), (0,)), ((), ())), preferred_element_type=jnp.float32)
            if b == 0:
                (one_high, one_low)[n][...] = picked.astype(jnp.bfloat16)
            else:
                two[n] = picked.astype(jnp.bfloat16)


def make_branches(firsts, right, labels, place, rows, cols):
    branches, bond, low_pairs = right.shape
    fetched = len(firsts) > 1
    return pl.pallas_call(
        functools.partial(branch_kernel, fetched),
        out_shape=[pltpu.VMEM((cols, rows), jnp.bfloat16)] * 2 + [pltpu.VMEM((2, rows, cols), jnp.bfloat16)],
        in_specs=[SMEM, SMEM] + [AWAY] * (len(firsts) + 1),
        out_specs=[VMEM] * 3,
        scratch_shapes=[
            pltpu.VMEM((rows * cols // (LOW * LOW), bond), jnp.float32),
            pltpu.VMEM((rows * cols // (LOW * LOW), low_pairs), jnp.float32),
            pltpu.VMEM((rows, cols), jnp.float32),
            pltpu.VMEM((branches, rows, rows), jnp.bfloat16),
            pltpu.VMEM(right.shape, right.dtype),
            pltpu.SemaphoreType.DMA((branches,)),
            *(pltpu.VMEM(x.shape, x.dtype) for x in firsts),
            pltpu.SemaphoreType.DMA((len(firsts),)),
        ],
        compiler_params=pltpu.CompilerParams(vmem_limit_bytes=LIMIT),
        name="branches",
    )(place, labels, *(off_chip(x) for x in firsts), off_chip(right))


def stem_kernel(stems, grps, steps, blocks, one_high, one_low, two, out_away, out, left):
    inner = blocks.shape[2]
    x = blocks[...].reshape(stems, grps, blocks.shape[1], inner)
    slab = jnp.concatenate([x[:, g].reshape(-1, inner) for g in range(grps)], axis=1)
    turned = split(dot3((one_high[...], one_low[...]), split(slab), ((1,), (1,))))
    sends, start = [], 0
    for n, size in enumerate(steps):
        rows = pl.ds(start, size)
        out[rows, :] = dot3(
            tuple(t[start : start + size] for t in turned), (two[0], two[1]), ((1,), (0,))
        )
        sends.append(pltpu.make_async_copy(out.at[rows], out_away.at[rows], left.at[n]))
        sends[-1].start()
        start += size
    for send in sends:
        send.wait()


def contract(blocks, parts, stems, grps):
    if blocks.shape[2] % LANES:
        x = blocks.reshape(stems, grps, *blocks.shape[1:])
        blocks = x.transpose(0, 2, 1, 3).reshape(stems, blocks.shape[1], -1)
        grps = 1
    one_high, one_low, two = parts
    shape = (one_high.shape[0], two.shape[2])
    steps = (shape[0] // 2, shape[0] // 4, shape[0] // 4)
    return pl.pallas_call(
        functools.partial(stem_kernel, stems, grps, steps),
        out_shape=jax.ShapeDtypeStruct(shape, jnp.float32),
        in_specs=[VMEM] * 4,
        out_specs=AWAY,
        scratch_shapes=[
            pltpu.VMEM(shape, jnp.float32),
            pltpu.SemaphoreType.DMA((len(steps),)),
        ],
        compiler_params=pltpu.CompilerParams(vmem_limit_bytes=LIMIT),
        name="contract",
    )(on_chip(blocks), on_chip(one_high), on_chip(one_low), on_chip(two))


def fetch(left, stems, grps):
    near = lax.ppermute(left, "grp", [(j, j ^ 1) for j in range(grps)])
    pairs = [(i * grps + j, i * grps + (j ^ (2 + i % 2))) for i in range(stems) for j in range(grps)]
    same = lax.ppermute(left, ("stem", "grp"), pairs)
    other = lax.ppermute(same, "stem", [(j, j ^ 1) for j in range(stems)])
    return left, near, same, other


def on_device(stem_tensor, left_factors, right_factors, index_labels):
    stems, grps = lax.axis_size("stem"), lax.axis_size("grp")
    s, g = lax.axis_index("stem"), lax.axis_index("grp")
    branches, p_part, upper, bond = left_factors.shape
    rows, cols = p_part * grps * LOW, upper * LOW
    if (stems % 2, grps) == (0, 4):
        firsts, cross = fetch(left_factors, stems, grps), g * p_part
    else:
        whole = lax.all_gather(left_factors, "grp", axis=1, tiled=True)
        firsts, cross = (whole.transpose(0, 2, 1, 3).reshape(branches, -1, bond),), 0 * g
    blocks = lax.all_to_all(stem_tensor, ("stem", "grp"), split_axis=0, concat_axis=0, tiled=True)
    place = jnp.stack([s, cross]).astype(jnp.int32)
    parts = make_branches(firsts, right_factors, index_labels, place, rows, cols)
    count = stem_tensor.shape[0] // (stems * grps)
    blocks = blocks.reshape(stems * grps, count, *stem_tensor.shape[1:])
    return jnp.stack([contract(blocks[:, o], parts, stems, grps) for o in range(count)])


def solution(mesh):
    placed = (P(None, "stem", "grp"), P(None, "grp", None, None), P(), P())
    return jax.shard_map(
        on_device,
        mesh=mesh,
        in_specs=placed,
        out_specs=P(("stem", "grp"), None, None),
        check_vma=False,
    )
```

time: 54.3 us -> 49.1 us (0.904)
  Pallas kernels: 10.6 us -> 8.26 us
  starting transfers between devices: 13.6 us -> 11.6 us
  waiting for transfers between devices: 29.6 us -> 29 us
    ppermute x4 -> x1, starting transfers between devices: 6.23 us -> 2.74 us  [fetch(): same = lax.ppermute(left, ('stem', 'grp'), pairs)]
    ppermute x1, starting transfers between devices: 0.01 us -> 1.51 us  [fetch(): near = lax.ppermute(left, 'grp', [(j, j ^ 1) for j in range(grps)])]
    ppermute x1, waiting for transfers between devices: 1.44 us -> 0.01 us  [fetch(): near = lax.ppermute(left, 'grp', [(j, j ^ 1) for j in range(grps)])]
    ppermute x1, waiting for transfers between devices: 0.01 us -> 1.4 us  [fetch(): other = lax.ppermute(same, 'stem', [(j, j ^ 1) for j in range(stems)])]
    pallas_call x1, Pallas kernels: 6.99 us -> 5.64 us  [make_branches(): pl.pallas_call(functools.partial(branch_kernel, fetched), out_shape=[pltp...]
    pallas_call x1, Pallas kernels: 3.64 us -> 2.61 us  [contract(): pl.pallas_call(functools.partial(stem_kernel, stems, grps, steps), out_sh...]
    ppermute x4 -> x1, waiting for transfers between devices: 28.1 us -> 27.6 us  [fetch(): same = lax.ppermute(left, ('stem', 'grp'), pairs)]
  transfers between devices with their start and end apart: 7 -> 4, of which waited for: 5 -> 2; matrix products, arithmetic and copies ran while one was open for 0% -> 0% of each run, Pallas kernels for 13% -> 12%
where the time goes in v3:
time: 49.1 us; the launch traced here: 48.9 us
  waiting for transfers between devices  29 us (59%)
  starting transfers between devices  11.6 us (24%)
  Pallas kernels  8.26 us (17%)
    ppermute x1, waiting for transfers between devices, fetch(): same = lax.ppermute(left, ('stem', 'grp'), pairs)  27.6 us
    all_to_all x1, starting transfers between devices, on_device(): lax.all_to_all(stem_tensor, ('stem', 'grp'), split_axis=0, concat_axis=0,...  7.33 us
    pallas_call x1, Pallas kernels, make_branches(): pl.pallas_call(functools.partial(branch_kernel, fetched), out_shape=[pltp...  5.64 us
    ppermute x1, starting transfers between devices, fetch(): same = lax.ppermute(left, ('stem', 'grp'), pairs)  2.74 us
    pallas_call x1, Pallas kernels, contract(): pl.pallas_call(functools.partial(stem_kernel, stems, grps, steps), out_sh...  2.61 us
    ppermute x1, starting transfers between devices, fetch(): near = lax.ppermute(left, 'grp', [(j, j ^ 1) for j in range(grps)])  1.51 us
    ppermute x1, waiting for transfers between devices, fetch(): other = lax.ppermute(same, 'stem', [(j, j ^ 1) for j in range(stems)])  1.4 us
  transfers between devices with their start and end apart: 4, of which 2 were waited for; matrix products, arithmetic and copies ran while one was open for 0% of the time, Pallas kernels for 12%

profile of v3, /device:TPU:0, one launch (start us, length us, event | category | flops | bytes accessed | tf_op | source)
XLA Modules:
  0.0 48.9 jit_solution(15425253541218649034)
XLA Ops:
  0.0 0.0 copy-start.1
  0.0 0.0 copy-start
  0.0 7.3 %all-to-all-start = ((f32[32,64,128]{2,1,0:T(8,128)}), f32[32,64,128]{2,1,0:T(8,128)S(1)}, u32[]{:S(2)}, u32[]{:S(2)}) async-start(f32[32,64,128]{2,1,0:T(8,128)} %param.4), calls=%async_computation | async-start | bytes 2097152 | tf_op jit(solution)/shard_map/all_to_all | solution.py:197
  7.3 0.0 copy-done.1
  7.3 2.7 %collective-permute-start.1 = (f32[2,4,16,256]{3,2,1,0:T(8,128)S(1)}, f32[2,4,16,256]{3,2,1,0:T(8,128)S(1)}, u32[]{:S(2)}, u32[]{:S(2)}) collective-permute-start(f32[2,4,16,256]{3,2,1,0:T(8,128)S(1)} %copy-done.1), channel_id=1, source_target_pairs={{0,2},{1,3},{2,0},{3,1},{4,7},{5,6},{6,5},{7,4},{8,10},{9,11},{10,... | collective-permute-start | bytes 393224 | tf_op jit(solution)/shard_map/ppermute | solution.py:182
  10.1 1.5 %collective-permute-start = (f32[2,4,16,256]{3,2,1,0:T(8,128)S(1)}, f32[2,4,16,256]{3,2,1,0:T(8,128)S(1)}, u32[]{:S(2)}, u32[]{:S(2)}) collective-permute-start(f32[2,4,16,256]{3,2,1,0:T(8,128)S(1)} %copy-done.1), channel_id=1, source_target_pairs={{0,1},{1,0},{2,3},{3,2},{4,5},{5,4},{6,7},{7,6},{8,9},{9,8},{10,11... | collective-permute-start | bytes 393224 | tf_op jit(solution)/shard_map/ppermute | solution.py:180
  11.6 27.6 %collective-permute-done.1.refs_2_ = f32[2,4,16,256]{3,2,1,0:T(8,128)S(1)} collective-permute-done((f32[2,4,16,256]{3,2,1,0:T(8,128)S(1)}, f32[2,4,16,256]{3,2,1,0:T(8,128)S(1)}, u32[]{:S(2)}, u32[]{:S(2)}) %collective-permute-start.1) | collective-permute-done | bytes 131104 | tf_op jit(solution)/shard_map/ppermute | solution.py:182
  39.2 0.0 copy-start.2
  39.2 0.0 collective-permute-start.2
  39.2 0.1 pad_add_fusion.place
  39.2 0.0 collective-permute-done.refs_1_
  39.2 0.0 copy-start.3
  39.2 1.4 %collective-permute-done.2.refs_3_ = f32[2,4,16,256]{3,2,1,0:T(8,128)} collective-permute-done((f32[2,4,16,256]{3,2,1,0:T(8,128)S(1)}, f32[2,4,16,256]{3,2,1,0:T(8,128)}, u32[]{:S(2)}, u32[]{:S(2)}) %collective-permute-start.2) | collective-permute-done | bytes 131104 | tf_op jit(solution)/shard_map/ppermute | solution.py:183
  40.6 0.0 copy-done.2
  40.6 0.0 copy-done.3
  40.6 0.0 copy-done
  40.7 5.6 %branches.1 = (bf16[512,512]{1,0:T(8,128)(2,1)S(1)}, bf16[512,512]{1,0:T(8,128)(2,1)S(1)}, bf16[2,512,512]{2,1,0:T(8,128)(2,1)S(1)}) custom-call(s32[2]{0:T(128)S(1)} %pad_add_fusion.place, s32[2,9]{1,0:T(2,128)S(1)} %copy-done, f32[2,4,16,256]{3,2,1,0:T(8,128)} %refs_0_.1, f32[2,4,16,256]{3,2,1,0:T(8,128)} %copy-done.3, f32[2,4,16,256]{3,2,1,0:T(8,128)} %copy-done.2, ...), custom_call_target="tpu_custom_call" | custom-call | tf_op jit(solution)/shard_map/branches/pallas_call | solution.py:119
  46.3 0.0 all-to-all-done.blocks
  46.3 2.6 %contract.1 = f32[512,512]{1,0:T(8,128)} custom-call(f32[32,64,128]{2,1,0:T(8,128)S(1)} %all-to-all-done.blocks, bf16[512,512]{1,0:T(8,128)(2,1)S(1)} %get-tuple-element.8.one_high, bf16[512,512]{1,0:T(8,128)(2,1)S(1)} %get-tuple-element.9.one_low, bf16[2,512,512]{2,1,0:T(8,128)(2,1)S(1)} %get-tuple-element.10.two), custom_call_target="tpu_custom_call" | custom-call | tf_op jit(solution)/shard_map/contract/pallas_call | solution.py:165
Async XLA Ops:
  0.0 7.3 %copy-start.1 = (f32[2,4,16,256]{3,2,1,0:T(8,128)S(1)}, f32[2,4,16,256]{3,2,1,0:T(8,128)}, u32[]{:S(2)}) copy-start(f32[2,4,16,256]{3,2,1,0:T(8,128)} %refs_0_.1) | copy-start | bytes 393220
  0.0 40.6 %copy-start = (s32[2,9]{1,0:T(2,128)S(1)}, s32[2,9]{1,0:T(2,128)}, u32[]{:S(2)}) copy-start(s32[2,9]{1,0:T(2,128)} %labels.1) | copy-start | bytes 220
  0.0 46.3 %all-to-all-start = ((f32[32,64,128]{2,1,0:T(8,128)}), f32[32,64,128]{2,1,0:T(8,128)S(1)}, u32[]{:S(2)}, u32[]{:S(2)}) async-start(f32[32,64,128]{2,1,0:T(8,128)} %param.4), calls=%async_computation | async-start | bytes 2097152 | tf_op jit(solution)/shard_map/all_to_all | solution.py:197
  7.3 31.8 %collective-permute-start.1 = (f32[2,4,16,256]{3,2,1,0:T(8,128)S(1)}, f32[2,4,16,256]{3,2,1,0:T(8,128)S(1)}, u32[]{:S(2)}, u32[]{:S(2)}) collective-permute-start(f32[2,4,16,256]{3,2,1,0:T(8,128)S(1)} %copy-done.1), channel_id=1, source_target_pairs={{0,2},{1,3},{2,0},{3,1},{4,7},{5,6},{6,5},{7,4},{8,10},{9,11},{10,... | collective-permute-start | bytes 393224 | tf_op jit(solution)/shard_map/ppermute | solution.py:182
  10.1 29.2 %collective-permute-start = (f32[2,4,16,256]{3,2,1,0:T(8,128)S(1)}, f32[2,4,16,256]{3,2,1,0:T(8,128)S(1)}, u32[]{:S(2)}, u32[]{:S(2)}) collective-permute-start(f32[2,4,16,256]{3,2,1,0:T(8,128)S(1)} %copy-done.1), channel_id=1, source_target_pairs={{0,1},{1,0},{2,3},{3,2},{4,5},{5,4},{6,7},{7,6},{8,9},{9,8},{10,11... | collective-permute-start | bytes 393224 | tf_op jit(solution)/shard_map/ppermute | solution.py:180
  39.2 1.5 %copy-start.2 = (f32[2,4,16,256]{3,2,1,0:T(8,128)}, f32[2,4,16,256]{3,2,1,0:T(8,128)S(1)}, u32[]{:S(2)}) copy-start(f32[2,4,16,256]{3,2,1,0:T(8,128)S(1)} %collective-permute-done.1.refs_2_) | copy-start | bytes 393220
  39.2 1.5 %collective-permute-start.2 = (f32[2,4,16,256]{3,2,1,0:T(8,128)S(1)}, f32[2,4,16,256]{3,2,1,0:T(8,128)}, u32[]{:S(2)}, u32[]{:S(2)}) collective-permute-start(f32[2,4,16,256]{3,2,1,0:T(8,128)S(1)} %collective-permute-done.1.refs_2_), channel_id=1, source_target_pairs={{0,4},{4,0},{8,12},{12,8},{16,20},{20,16},{24,28},{28,24},{1,5},{5... | collective-permute-start | bytes 393224 | tf_op jit(solution)/shard_map/ppermute | solution.py:183
  39.2 1.4 %copy-start.3 = (f32[2,4,16,256]{3,2,1,0:T(8,128)}, f32[2,4,16,256]{3,2,1,0:T(8,128)S(1)}, u32[]{:S(2)}) copy-start(f32[2,4,16,256]{3,2,1,0:T(8,128)S(1)} %collective-permute-done.refs_1_) | copy-start | bytes 393220

commit v4 on v3

--- a/solution.py
+++ b/solution.py
@@ -38,13 +38,19 @@
     return one(a_high, b_high) + (one(a_high, b_low) + one(a_low, b_high))
 
 
-def order_rows(place, own, near, same, other, ordered, b):
+def order_rows(place, own, first, swapped, second, passed, ordered, b):
     _, p_part, upper, _ = own.shape
     core = jnp.bitwise_and(place[0], 1)
     per_u = 4 * p_part
     for p in range(p_part):
-        mine, its = same[b, p], other[b, p]
-        for n, rows in enumerate((own[b, p], near[b, p], jnp.where(core == 0, mine, its), jnp.where(core == 0, its, mine))):
+        mine, its = first[b, p], swapped[b, p]
+        slots = (
+            own[b, p],
+            jnp.where(core == 1, mine, its),
+            jnp.where(core == 1, its, mine),
+            jnp.where(core == 1, passed[b, p], second[b, p]),
+        )
+        for n, rows in enumerate(slots):
             for u in range(upper):
                 ordered[pl.ds(u * per_u + n * p_part + p, 1), :] = rows[u : u + 1]
 
@@ -62,7 +68,7 @@
 
 
 def branch_kernel(fetched, place, labels, *refs):
-    count = 4 if fetched else 1
+    count = 5 if fetched else 1
     away, refs = refs[:count], refs[count:]
     right_away, one_high, one_low, two, ordered, product, wide, chosen, right, arrived = refs[:10]
     near_by, here = refs[10:-1], refs[-1]
@@ -83,6 +89,7 @@
         for j in range(labels.shape[1]):
             source = source + jnp.left_shift(jnp.bitwise_and(jnp.right_shift(to_id, j), 1), labels[b, j])
         upper = jnp.bitwise_xor(jnp.right_shift(source, LOW.bit_length() - 1), place[1])
+        upper = jnp.where(upper >= upper_p // 2, jnp.bitwise_xor(upper, place[2]), upper)
         source = jnp.bitwise_and(source, LOW - 1) * upper_p + upper
         chosen[b] = (from_id == source).astype(jnp.float32).astype(jnp.bfloat16)
     for take in takes:
@@ -161,7 +168,7 @@
         grps = 1
     one_high, one_low, two = parts
     shape = (one_high.shape[0], two.shape[2])
-    steps = (shape[0] // 2, shape[0] // 4, shape[0] // 4)
+    steps = (shape[0] * 3 // 4, shape[0] // 4)
     return pl.pallas_call(
         functools.partial(stem_kernel, stems, grps, steps),
         out_shape=jax.ShapeDtypeStruct(shape, jnp.float32),
@@ -177,11 +184,13 @@
 
 
 def fetch(left, stems, grps):
-    near = lax.ppermute(left, "grp", [(j, j ^ 1) for j in range(grps)])
-    pairs = [(i * grps + j, i * grps + (j ^ (2 + i % 2))) for i in range(stems) for j in range(grps)]
-    same = lax.ppermute(left, ("stem", "grp"), pairs)
-    other = lax.ppermute(same, "stem", [(j, j ^ 1) for j in range(stems)])
-    return left, near, same, other
+    offsets = [1 if i % 2 else 2 + i // 2 % 2 for i in range(stems)]
+    pairs = [(i * grps + j, i * grps + (j ^ offsets[i])) for i in range(stems) for j in range(grps)]
+    first = lax.ppermute(left, ("stem", "grp"), pairs)
+    swapped = lax.ppermute(first, "stem", [(j, j ^ 1) for j in range(stems)])
+    second = lax.ppermute(first, "stem", [(j, j ^ 2) for j in range(0, stems, 2)])
+    passed = lax.ppermute(second, "stem", [(j, j ^ 1) for j in range(0, stems, 2)])
+    return left, first, swapped, second, passed
 
 
 def on_device(stem_tensor, left_factors, right_factors, index_labels):
@@ -189,13 +198,13 @@
     s, g = lax.axis_index("stem"), lax.axis_index("grp")
     branches, p_part, upper, bond = left_factors.shape
     rows, cols = p_part * grps * LOW, upper * LOW
-    if (stems % 2, grps) == (0, 4):
-        firsts, cross = fetch(left_factors, stems, grps), g * p_part
+    if (stems % 4, grps) == (0, 4):
+        firsts, cross, trade = fetch(left_factors, stems, grps), g * p_part, s // 2 % 2 * p_part
     else:
         whole = lax.all_gather(left_factors, "grp", axis=1, tiled=True)
-        firsts, cross = (whole.transpose(0, 2, 1, 3).reshape(branches, -1, bond),), 0 * g
+        firsts, cross, trade = (whole.transpose(0, 2, 1, 3).reshape(branches, -1, bond),), 0 * g, 0 * s
     blocks = lax.all_to_all(stem_tensor, ("stem", "grp"), split_axis=0, concat_axis=0, tiled=True)
-    place = jnp.stack([s, cross]).astype(jnp.int32)
+    place = jnp.stack([s, cross, trade]).astype(jnp.int32)
     parts = make_branches(firsts, right_factors, index_labels, place, rows, cols)
     count = stem_tensor.shape[0] // (stems * grps)
     blocks = blocks.reshape(stems * grps, count, *stem_tensor.shape[1:])

time: 49.1 us -> 54.5 us (1.11)
  waiting for transfers between devices: 29 us -> 31.5 us
  starting transfers between devices: 11.6 us -> 14 us
    ppermute x3 -> x4, waiting for transfers between devices: 29 us -> 31.5 us  [the longest x1 26.3 us: fetch(): first = lax.ppermute(left, ('stem', 'grp'), pairs)]
    ppermute x3 -> x4, starting transfers between devices: 4.25 us -> 6.66 us  [the longest x1 2.74 us: fetch(): first = lax.ppermute(left, ('stem', 'grp'), pairs)]
  transfers between devices with their start and end apart: 4 -> 5, of which waited for: 2 -> 3; matrix products, arithmetic and copies ran while one was open for 0% -> 0% of each run, Pallas kernels for 12% -> 11%
where the time goes in v4:
time: 54.5 us; the launch traced here: 54.2 us
  waiting for transfers between devices  31.5 us (58%)
  starting transfers between devices  14 us (26%)
  Pallas kernels  8.34 us (15%)
    ppermute x1, waiting for transfers between devices, fetch(): first = lax.ppermute(left, ('stem', 'grp'), pairs)  26.3 us
    all_to_all x1, starting transfers between devices, on_device(): lax.all_to_all(stem_tensor, ('stem', 'grp'), split_axis=0, concat_axis=0,...  7.33 us
    pallas_call x1, Pallas kernels, make_branches(): pl.pallas_call(functools.partial(branch_kernel, fetched), out_shape=[pltp...  5.7 us
    ppermute x1, waiting for transfers between devices, fetch(): lax.ppermute(first, 'stem', [(j, j ^ 2) for j in range(0, stems, 2)])  4.85 us
    ppermute x1, starting transfers between devices, fetch(): first = lax.ppermute(left, ('stem', 'grp'), pairs)  2.74 us
    pallas_call x1, Pallas kernels, contract(): pl.pallas_call(functools.partial(stem_kernel, stems, grps, steps), out_sh...  2.64 us
    ppermute x1, starting transfers between devices, fetch(): lax.ppermute(second, 'stem', [(j, j ^ 1) for j in range(0, stems, 2)])  1.94 us
    ppermute x1, starting transfers between devices, fetch(): lax.ppermute(first, 'stem', [(j, j ^ 2) for j in range(0, stems, 2)])  1.91 us
  transfers between devices with their start and end apart: 5, of which 3 were waited for; matrix products, arithmetic and copies ran while one was open for 0% of the time, Pallas kernels for 11%

profile of v4, /device:TPU:0, one launch (start us, length us, event | category | flops | bytes accessed | tf_op | source)
XLA Modules:
  0.0 54.2 jit_solution(2833907886884810778)
XLA Ops:
  0.0 0.0 copy-start.1
  0.0 0.0 copy-start
  0.0 7.3 %all-to-all-start = ((f32[32,64,128]{2,1,0:T(8,128)}), f32[32,64,128]{2,1,0:T(8,128)S(1)}, u32[]{:S(2)}, u32[]{:S(2)}) async-start(f32[32,64,128]{2,1,0:T(8,128)} %param.4), calls=%async_computation | async-start | bytes 2097152 | tf_op jit(solution)/shard_map/all_to_all | solution.py:206
  7.3 0.0 copy-done.1
  7.3 2.7 %collective-permute-start = (f32[2,4,16,256]{3,2,1,0:T(8,128)S(1)}, f32[2,4,16,256]{3,2,1,0:T(8,128)S(1)}, u32[]{:S(2)}, u32[]{:S(2)}) collective-permute-start(f32[2,4,16,256]{3,2,1,0:T(8,128)S(1)} %copy-done.1), channel_id=1, source_target_pairs={{0,2},{1,3},{2,0},{3,1},{4,5},{5,4},{6,7},{7,6},{8,11},{9,10},{10,... | collective-permute-start | bytes 393224 | tf_op jit(solution)/shard_map/ppermute | solution.py:189
  10.1 26.3 %collective-permute-done.refs_1_ = f32[2,4,16,256]{3,2,1,0:T(8,128)S(1)} collective-permute-done((f32[2,4,16,256]{3,2,1,0:T(8,128)S(1)}, f32[2,4,16,256]{3,2,1,0:T(8,128)S(1)}, u32[]{:S(2)}, u32[]{:S(2)}) %collective-permute-start) | collective-permute-done | bytes 131104 | tf_op jit(solution)/shard_map/ppermute | solution.py:189
  36.4 0.0 copy-start.2
  36.4 1.9 %collective-permute-start.2 = (f32[2,4,16,256]{3,2,1,0:T(8,128)S(1)}, f32[2,4,16,256]{3,2,1,0:T(8,128)S(1)}, u32[]{:S(2)}, u32[]{:S(2)}) collective-permute-start(f32[2,4,16,256]{3,2,1,0:T(8,128)S(1)} %collective-permute-done.refs_1_), channel_id=1, source_target_pairs={{0,8},{8,0},{16,24},{24,16},{1,9},{9,1},{17,25},{25,17},{2,10},{10... | collective-permute-start | bytes 393224 | tf_op jit(solution)/shard_map/ppermute | solution.py:191
  38.3 0.1 collective-permute-start.1
  38.3 4.9 %collective-permute-done.2.refs_3_ = f32[2,4,16,256]{3,2,1,0:T(8,128)S(1)} collective-permute-done((f32[2,4,16,256]{3,2,1,0:T(8,128)S(1)}, f32[2,4,16,256]{3,2,1,0:T(8,128)S(1)}, u32[]{:S(2)}, u32[]{:S(2)}) %collective-permute-start.2) | collective-permute-done | bytes 131104 | tf_op jit(solution)/shard_map/ppermute | solution.py:191
  43.2 0.0 copy-start.3
  43.2 1.9 %collective-permute-start.3 = (f32[2,4,16,256]{3,2,1,0:T(8,128)S(1)}, f32[2,4,16,256]{3,2,1,0:T(8,128)}, u32[]{:S(2)}, u32[]{:S(2)}) collective-permute-start(f32[2,4,16,256]{3,2,1,0:T(8,128)S(1)} %collective-permute-done.2.refs_3_), channel_id=1, source_target_pairs={{0,4},{8,12},{16,20},{24,28},{1,5},{9,13},{17,21},{25,29},{2,6},{1... | collective-permute-start | bytes 393224 | tf_op jit(solution)/shard_map/ppermute | solution.py:192
  45.1 0.1 pad_add_fusion.place
  45.2 0.0 collective-permute-done.1.refs_2_
  45.2 0.0 copy-start.4
  45.2 0.4 collective-permute-done.3.refs_4_
  45.6 0.0 copy-done.2
  45.6 0.0 copy-done.3
  45.6 0.3 copy-done.4
  45.9 0.0 copy-done
  45.9 5.7 %branches.1 = (bf16[512,512]{1,0:T(8,128)(2,1)S(1)}, bf16[512,512]{1,0:T(8,128)(2,1)S(1)}, bf16[2,512,512]{2,1,0:T(8,128)(2,1)S(1)}) custom-call(s32[3]{0:T(128)S(1)} %pad_add_fusion.place, s32[2,9]{1,0:T(2,128)S(1)} %copy-done, f32[2,4,16,256]{3,2,1,0:T(8,128)} %refs_0_.1, f32[2,4,16,256]{3,2,1,0:T(8,128)} %copy-done.2, f32[2,4,16,256]{3,2,1,0:T(8,128)} %copy-done.4, ...), custom_call_target="tpu_custom_call" | custom-call | tf_op jit(solution)/shard_map/branches/pallas_call | solution.py:126
  51.6 0.0 all-to-all-done.blocks
  51.6 2.6 %contract.1 = f32[512,512]{1,0:T(8,128)} custom-call(f32[32,64,128]{2,1,0:T(8,128)S(1)} %all-to-all-done.blocks, bf16[512,512]{1,0:T(8,128)(2,1)S(1)} %get-tuple-element.8.one_high, bf16[512,512]{1,0:T(8,128)(2,1)S(1)} %get-tuple-element.9.one_low, bf16[2,512,512]{2,1,0:T(8,128)(2,1)S(1)} %get-tuple-element.10.two), custom_call_target="tpu_custom_call" | custom-call | tf_op jit(solution)/shard_map/contract/pallas_call | solution.py:172
Async XLA Ops:
  0.0 7.3 %copy-start.1 = (f32[2,4,16,256]{3,2,1,0:T(8,128)S(1)}, f32[2,4,16,256]{3,2,1,0:T(8,128)}, u32[]{:S(2)}) copy-start(f32[2,4,16,256]{3,2,1,0:T(8,128)} %refs_0_.1) | copy-start | bytes 393220
  0.0 45.9 %copy-start = (s32[2,9]{1,0:T(2,128)S(1)}, s32[2,9]{1,0:T(2,128)}, u32[]{:S(2)}) copy-start(s32[2,9]{1,0:T(2,128)} %labels.1) | copy-start | bytes 220
  0.0 51.6 %all-to-all-start = ((f32[32,64,128]{2,1,0:T(8,128)}), f32[32,64,128]{2,1,0:T(8,128)S(1)}, u32[]{:S(2)}, u32[]{:S(2)}) async-start(f32[32,64,128]{2,1,0:T(8,128)} %param.4), calls=%async_computation | async-start | bytes 2097152 | tf_op jit(solution)/shard_map/all_to_all | solution.py:206
  7.3 29.0 %collective-permute-start = (f32[2,4,16,256]{3,2,1,0:T(8,128)S(1)}, f32[2,4,16,256]{3,2,1,0:T(8,128)S(1)}, u32[]{:S(2)}, u32[]{:S(2)}) collective-permute-start(f32[2,4,16,256]{3,2,1,0:T(8,128)S(1)} %copy-done.1), channel_id=1, source_target_pairs={{0,2},{1,3},{2,0},{3,1},{4,5},{5,4},{6,7},{7,6},{8,11},{9,10},{10,... | collective-permute-start | bytes 393224 | tf_op jit(solution)/shard_map/ppermute | solution.py:189
  36.4 9.2 %copy-start.2 = (f32[2,4,16,256]{3,2,1,0:T(8,128)}, f32[2,4,16,256]{3,2,1,0:T(8,128)S(1)}, u32[]{:S(2)}) copy-start(f32[2,4,16,256]{3,2,1,0:T(8,128)S(1)} %collective-permute-done.refs_1_) | copy-start | bytes 393220
  36.4 6.8 %collective-permute-start.2 = (f32[2,4,16,256]{3,2,1,0:T(8,128)S(1)}, f32[2,4,16,256]{3,2,1,0:T(8,128)S(1)}, u32[]{:S(2)}, u32[]{:S(2)}) collective-permute-start(f32[2,4,16,256]{3,2,1,0:T(8,128)S(1)} %collective-permute-done.refs_1_), channel_id=1, source_target_pairs={{0,8},{8,0},{16,24},{24,16},{1,9},{9,1},{17,25},{25,17},{2,10},{10... | collective-permute-start | bytes 393224 | tf_op jit(solution)/shard_map/ppermute | solution.py:191
  38.3 7.0 %collective-permute-start.1 = (f32[2,4,16,256]{3,2,1,0:T(8,128)S(1)}, f32[2,4,16,256]{3,2,1,0:T(8,128)S(1)}, u32[]{:S(2)}, u32[]{:S(2)}) collective-permute-start(f32[2,4,16,256]{3,2,1,0:T(8,128)S(1)} %collective-permute-done.refs_1_), channel_id=1, source_target_pairs={{0,4},{4,0},{8,12},{12,8},{16,20},{20,16},{24,28},{28,24},{1,5},{5... | collective-permute-start | bytes 393224 | tf_op jit(solution)/shard_map/ppermute | solution.py:190
  43.2 2.4 %copy-start.3 = (f32[2,4,16,256]{3,2,1,0:T(8,128)}, f32[2,4,16,256]{3,2,1,0:T(8,128)S(1)}, u32[]{:S(2)}) copy-start(f32[2,4,16,256]{3,2,1,0:T(8,128)S(1)} %collective-permute-done.2.refs_3_) | copy-start | bytes 393220
  43.2 2.4 %collective-permute-start.3 = (f32[2,4,16,256]{3,2,1,0:T(8,128)S(1)}, f32[2,4,16,256]{3,2,1,0:T(8,128)}, u32[]{:S(2)}, u32[]{:S(2)}) collective-permute-start(f32[2,4,16,256]{3,2,1,0:T(8,128)S(1)} %collective-permute-done.2.refs_3_), channel_id=1, source_target_pairs={{0,4},{8,12},{16,20},{24,28},{1,5},{9,13},{17,21},{25,29},{2,6},{1... | collective-permute-start | bytes 393224 | tf_op jit(solution)/shard_map/ppermute | solution.py:192
  45.2 0.7 %copy-start.4 = (f32[2,4,16,256]{3,2,1,0:T(8,128)}, f32[2,4,16,256]{3,2,1,0:T(8,128)S(1)}, u32[]{:S(2)}) copy-start(f32[2,4,16,256]{3,2,1,0:T(8,128)S(1)} %collective-permute-done.1.refs_2_) | copy-start | bytes 393220
